TPU v7x, 128 devices: a whole 4x4x4 slice. The times are simulated.
128 devices in a mesh: row: 16 (over x_hi, z, core), col: 8 (over y, x_lo).
Axes of the slice: x: 4 (x_hi: 2, x_lo: 2; x = x_hi * 2 + x_lo), y: 4, z: 4, core: 2. Of those that a mesh axis runs over, the one named last changes fastest.
Arguments:
- buoy: bfloat16 [512, 512, 384], P('row', 'col'), may hold values from -6 to 6
- vel_w: bfloat16 [512, 512, 384], P('row', 'col'), may hold values from -6 to 6
- strat: float32 [576], P('col'), may hold values from 0.3 to 3
- eig_val: float32 [384], replicated, may hold values from 0.1 to 8
- eig_left: bfloat16 [384, 384], replicated, may hold values from -0.3125 to 0.3125
- eig_right: bfloat16 [384, 384], replicated, may hold values from -0.3125 to 0.3125
Outputs:
- new_buoy: bfloat16 [512, 512, 384], P('row', 'col')
- new_vel: bfloat16 [512, 512, 384], P('row', 'col')
All inputs are finite; a program needn't handle non-finite values.
Results may differ from a plain program's by a relative error of at most 0.019.
The roundings to bfloat16 on the way count: a program that leaves them out, or rounds other values in their place, can miss the bound.
Values may be sent and summed in bfloat16 or wider, within the bound.
A program may use at most 128 MiB of HBM per device.

v0:
```python
import math

import jax
import jax.numpy as jnp
from jax import lax
from jax.sharding import PartitionSpec as P

KX = 512
KY = 512
NZ = 384
XG = 768
YG = 768
ZG = 576


explicit_step = 0.5
diffuse_buoy = 0.5
diffuse_vel = 0.25
couple_buoy = 0.7
couple_vel = 0.7


def fourier_trig(modes, points):
    order = jnp.arange(modes, dtype=jnp.int32)
    freq = ((order + 1) // 2).astype(jnp.float32)
    place = jnp.arange(points, dtype=jnp.float32)
    angle = 2.0 * math.pi / points * freq[:, None] * place[None, :]
    return (order, jnp.where((order % 2 == 0)[:, None], jnp.cos(angle), jnp.sin(angle)))


def fourier_eval(modes, points):
    order, values = fourier_trig(modes, points)
    return (values * math.sqrt(2.0 / modes)).astype(jnp.bfloat16)


def fourier_proj(modes, points):
    order, values = fourier_trig(modes, points)
    weight = jnp.where(order == 0, 1.0 / points, 2.0 / points).astype(jnp.float32)
    return jnp.transpose(values * weight[:, None] * math.sqrt(modes / 2.0)).astype(jnp.bfloat16)


def cheb_tables(degree, points):
    order = jnp.arange(degree, dtype=jnp.float32)
    theta = math.pi * (jnp.arange(points, dtype=jnp.float32) + 0.5) / points
    angle = order[:, None] * theta[None, :]
    norm = math.sqrt(2.0 / degree)
    levels = jnp.cos(angle) * norm
    slopes = -(order[:, None] / degree) * jnp.sin(angle) * norm
    weight = jnp.where(order == 0, 1.0 / points, 2.0 / points).astype(jnp.float32)
    projector = jnp.transpose(jnp.cos(angle) * weight[:, None] * math.sqrt(degree / 2.0))
    return (
        levels.astype(jnp.bfloat16),
        slopes.astype(jnp.bfloat16),
        projector.astype(jnp.bfloat16),
    )


def wave_squares(modes, offset, count):
    order = offset + jnp.arange(count, dtype=jnp.int32)
    freq = ((order + 1) // 2).astype(jnp.float32) * (2.0 / modes)
    return freq * freq


def lift_depth(coeffs, lookup, col_count):
    values = jnp.einsum("akn,nz->zak", coeffs, lookup, preferred_element_type=jnp.float32)
    return values.astype(jnp.bfloat16).reshape(col_count, values.shape[0] // col_count, -1)


def spread_rows(arrived, along_y, modes_x, modes_y, col_count, row_count):
    fields = arrived.shape[0]
    depth_part = arrived.shape[2]
    parts = arrived.reshape(fields, depth_part, col_count, modes_x, modes_y)
    result = jnp.einsum("fzcak,ckbi->fbaiz", parts, along_y, preferred_element_type=jnp.float32)
    return result.astype(jnp.bfloat16).reshape(fields, row_count, modes_x, -1)


def finish_grid(arrived, along_x):
    fields = arrived.shape[0]
    flat = arrived.reshape(fields, arrived.shape[2], arrived.shape[3])
    return jnp.einsum("fap,ax->fpx", flat, along_x, preferred_element_type=jnp.float32).astype(
        jnp.bfloat16
    )


def make_fluxes(vel_grid, slope_grid, strata_tiled):
    velocity = vel_grid.astype(jnp.float32)
    gradient = slope_grid.astype(jnp.float32)
    flux_buoy = -(velocity * gradient) - strata_tiled[:, None] * velocity
    flux_vel = -(velocity * jnp.abs(velocity))
    return jnp.stack([flux_buoy, flux_vel]).astype(jnp.bfloat16)


def fold_x(fluxes, back_x, row_count):
    values = jnp.einsum("fpx,xa->fap", fluxes, back_x, preferred_element_type=jnp.float32)
    fields, total_x, points = values.shape
    return values.astype(jnp.bfloat16).reshape(fields, row_count, total_x // row_count, points)


def fold_y(arrived, back_y, span_y, depth_part, col_count):
    fields, row_count, modes_x, points = arrived.shape
    parts = arrived.reshape(fields, row_count, modes_x, span_y, depth_part)
    values = jnp.einsum("fbaiz,bick->fczak", parts, back_y, preferred_element_type=jnp.float32)
    return values.astype(jnp.bfloat16).reshape(fields, col_count, depth_part, -1)


def fold_depth(arrived, projector, modes_x, modes_y):
    fields = arrived.shape[0]
    parts = arrived.reshape(fields, arrived.shape[1] * arrived.shape[2], modes_x, modes_y)
    return jnp.einsum("fzak,zn->fakn", parts, projector, preferred_element_type=jnp.float32)


def per_device(buoy, vel_w, strat, eig_val, eig_left, eig_right):
    row_count = lax.axis_size("row")
    col_count = lax.axis_size("col")
    modes_x, modes_y, degree = buoy.shape
    depth_part = ZG // col_count
    span_y = YG // row_count
    levels, slopes, projector = cheb_tables(NZ, ZG)
    along_y = fourier_eval(KY, YG).reshape(col_count, modes_y, row_count, span_y)
    along_x = fourier_eval(KX, XG)
    back_x = fourier_proj(KX, XG)
    back_y = fourier_proj(KY, YG).reshape(row_count, span_y, col_count, modes_y)
    strata_tiled = jnp.tile(strat, span_y)
    lifted = jnp.stack([lift_depth(vel_w, levels, col_count), lift_depth(buoy, slopes, col_count)])
    arrived = lax.all_to_all(lifted, "col", split_axis=1, concat_axis=3, tiled=True)
    spread = spread_rows(arrived, along_y, modes_x, modes_y, col_count, row_count)
    grid_all = finish_grid(
        lax.all_to_all(spread, "row", split_axis=1, concat_axis=2, tiled=True), along_x
    )
    fluxes = make_fluxes(grid_all[0], grid_all[1], strata_tiled)
    folded = lax.all_to_all(
        fold_x(fluxes, back_x, row_count), "row", split_axis=1, concat_axis=1, tiled=True
    )
    returned = lax.all_to_all(
        fold_y(folded, back_y, span_y, depth_part, col_count),
        "col",
        split_axis=1,
        concat_axis=1,
        tiled=True,
    )
    tendency = fold_depth(returned, projector, modes_x, modes_y)
    tend_buoy = tendency[0]
    tend_vel = tendency[1]
    rhs_buoy = (buoy.astype(jnp.float32) + explicit_step * tend_buoy).astype(jnp.bfloat16)
    rhs_vel = (vel_w.astype(jnp.float32) + explicit_step * tend_vel).astype(jnp.bfloat16)
    modal_buoy = jnp.einsum("akn,nj->akj", rhs_buoy, eig_left, preferred_element_type=jnp.float32)
    modal_vel = jnp.einsum("akn,nj->akj", rhs_vel, eig_left, preferred_element_type=jnp.float32)
    wave_x = wave_squares(KX, lax.axis_index("row") * modes_x, modes_x)
    wave_y = wave_squares(KY, lax.axis_index("col") * modes_y, modes_y)
    lapl = 4.0 * (wave_x[:, None, None] + wave_y[None, :, None]) + eig_val[None, None, :]
    diag_buoy = 1.0 + diffuse_buoy * lapl
    diag_vel = 1.0 + diffuse_vel * lapl
    determ = diag_buoy * diag_vel + couple_buoy * couple_vel
    solved_buoy = ((diag_vel * modal_buoy - couple_buoy * modal_vel) / determ).astype(jnp.bfloat16)
    solved_vel = ((diag_buoy * modal_vel + couple_vel * modal_buoy) / determ).astype(jnp.bfloat16)
    new_buoy = jnp.einsum(
        "akj,jn->akn", solved_buoy, eig_right, preferred_element_type=jnp.float32
    ).astype(jnp.bfloat16)
    new_vel = jnp.einsum(
        "akj,jn->akn", solved_vel, eig_right, preferred_element_type=jnp.float32
    ).astype(jnp.bfloat16)
    return (new_buoy, new_vel)


def solution(mesh):
    in_specs = (P("row", "col", None), P("row", "col", None), P("col"), P(), P(), P())
    out_specs = (P("row", "col", None), P("row", "col", None))
    return jax.shard_map(
        per_device, mesh=mesh, in_specs=in_specs, out_specs=out_specs, check_vma=False
    )
```

profile of v0, /device:TPU:100, one launch (start us, length us, event | category | flops | bytes accessed | tf_op | source)
XLA Modules:
  0.0 623.3 jit_solution(10420502041353524387)
XLA Ops:
  0.7 5.7 convolution_convert_fusion.1
  22.2 7.6 %pad_maximum_fusion = bf16[2,8,72,2048]{2,1,3,0:T(8,128)(2,1)} fusion(bf16[1,8,72,2048]{2,1,3,0:T(8,128)(2,1)} %stack_reshape.7, bf16[1,8,72,2048]{2,1,3,0:T(8,128)(2,1)} %stack_reshape.6), kind=kLoop, calls=%fused_computation.17 | loop fusion | flops 2359296 | bytes 9437184 | tf_op jit(solution)/shard_map/stack | solution.py:124
  29.8 11.4 %copy.17 = bf16[2,8,72,2048]{3,2,0,1:T(8,128)(2,1)} copy(bf16[2,8,72,2048]{2,1,3,0:T(8,128)(2,1)} %pad_maximum_fusion) | data formatting | bytes 9437184 | tf_op jit(solution)/shard_map/stack | solution.py:124
  46.7 55.0 %all-to-all-done = bf16[2,8,72,2048]{3,2,0,1:T(8,128)(2,1)} async-done(((bf16[2,8,72,2048]{3,2,0,1:T(8,128)(2,1)}), bf16[2,8,72,2048]{3,2,0,1:T(8,128)(2,1)}, u32[]{:S(2)}, u32[]{:S(2)}) %all-to-all-start) | async-done | bytes 4718624 | tf_op jit(solution)/shard_map/all_to_all | solution.py:125
  101.7 14.5 %reshape.246 = bf16[2,72,8,32,64]{4,3,1,0,2:T(8,128)(2,1)} reshape(bf16[2,1,72,8,2048]{4,2,0,3,1:T(8,128)(2,1)} %bitcast.8) | data formatting | bytes 9437184 | tf_op jit(solution)/shard_map/reshape | solution.py:72
  116.2 14.8 %copy.19 = bf16[2,72,8,32,64]{1,4,2,3,0:T(8,128)(2,1)} copy(bf16[2,72,8,32,64]{4,3,1,0,2:T(8,128)(2,1)} %reshape.246) | data formatting | bytes 9437184 | tf_op jit(solution)/shard_map/reshape | solution.py:72
  131.1 23.5 %fusion = bf16[2,16,32,48,72]{4,3,2,0,1:T(8,128)(2,1)} fusion(bf16[2,72,8,32,64]{1,4,2,3,0:T(8,128)(2,1)} %copy.19, f32[16,48]{1,0:T(8,128)S(1)} %multiply_add_fusion, f32[8,64]{1,0:T(8,128)S(1)} %fusion.93, pred[8,64]{1,0:T(8,128)(4,1)S(1)} %fusion.90), kind=kOutput, calls=%fused_computation.6 | convolution fusion | flops 3628990464 | bytes 11802112 | tf_op jit(solution)/shard_map/fzcak,ckbi->fbaiz/dot_general | solution.py:73
  154.6 20.2 %reshape.227 = bf16[2,16,32,3456]{3,2,0,1:T(8,128)(2,1)} reshape(bf16[2,16,32,48,72]{4,3,2,0,1:T(8,128)(2,1)} %fusion) | data formatting | bytes 14155776 | tf_op jit(solution)/shard_map/reshape | solution.py:74
  174.7 7.1 %all-to-all-start.1 = ((bf16[2,16,32,3456]{3,2,0,1:T(8,128)(2,1)}), bf16[2,16,32,3456]{3,2,0,1:T(8,128)(2,1)}, u32[]{:S(2)}, u32[]{:S(2)}) async-start(bf16[2,16,32,3456]{3,2,0,1:T(8,128)(2,1)} %reshape.227), calls=%async_computation.1 | async-start | bytes 14155776 | tf_op jit(solution)/shard_map/all_to_all | solution.py:128
  181.9 106.6 %all-to-all-done.1 = bf16[2,16,32,3456]{3,2,0,1:T(8,128)(2,1)} async-done(((bf16[2,16,32,3456]{3,2,0,1:T(8,128)(2,1)}), bf16[2,16,32,3456]{3,2,0,1:T(8,128)(2,1)}, u32[]{:S(2)}, u32[]{:S(2)}) %all-to-all-start.1) | async-done | bytes 7077920 | tf_op jit(solution)/shard_map/all_to_all | solution.py:128
  292.2 12.0 %convolution_convert_fusion = bf16[2,3456,768]{2,1,0:T(8,128)(2,1)S(1)} fusion(bf16[2,512,3456]{2,1,0:T(8,128)(2,1)S(1)} %bitcast.101, f32[512]{0:T(512)S(1)} %get-tuple-element.4, pred[512]{0:T(512)(128)(4,1)S(1)} %fusion.103), kind=kOutput, calls=%fused_computation.16 | convolution fusion | flops 5442699264 | bytes 17697280 | tf_op jit(solution)/shard_map/fap,ax->fpx/dot_general | solution.py:80
  304.2 6.6 %fusion.3 = (bf16[1,3456,768]{2,1,0:T(8,128)(2,1)}, bf16[1,3456,768]{2,1,0:T(8,128)(2,1)}) fusion(bf16[2,3456,768]{2,1,0:T(8,128)(2,1)S(1)} %convolution_convert_fusion, f32[3456]{0:T(1024)S(1)} %mul.326), kind=kLoop, calls=%fused_computation.9 | loop fusion | flops 29196288 | bytes 21247488 | tf_op jit(solution)/shard_map/convert
  310.9 18.2 %fusion.11 = bf16[512,2,3456]{2,0,1:T(8,128)(2,1)} fusion(bf16[1,3456,768]{2,1,0:T(8,128)(2,1)} %get-tuple-element.3, bf16[1,3456,768]{2,1,0:T(8,128)(2,1)} %get-tuple-element.2, f32[512]{0:T(512)S(1)} %get-tuple-element.5, f32[512]{0:T(512)S(1)} %get-tuple-element.4, pred[512]{0:T(512)(128)(4,1)S(1)} %fusion.103), kind=kOutput, calls=%fused_computation.19 | convolution fusion | flops 5462556672 | bytes 17699328 | tf_op jit(solution)/shard_map/fpx,xa->fap/dot_general | solution.py:94
  329.1 6.9 %copy.22 = bf16[2,16,32,3456]{3,2,0,1:T(8,128)(2,1)} copy(bf16[2,16,32,3456]{3,2,1,0:T(8,128)(2,1)} %bitcast.100) | data formatting | bytes 14155776 | tf_op jit(solution)/shard_map/reshape | solution.py:96
  335.9 7.2 %all-to-all-start.2 = ((bf16[2,16,32,3456]{3,2,0,1:T(8,128)(2,1)}), bf16[2,16,32,3456]{3,2,0,1:T(8,128)(2,1)}, u32[]{:S(2)}, u32[]{:S(2)}) async-start(bf16[2,16,32,3456]{3,2,0,1:T(8,128)(2,1)} %copy.22), calls=%async_computation.2 | async-start | bytes 14155776 | tf_op jit(solution)/shard_map/all_to_all | solution.py:131
  343.2 106.7 %all-to-all-done.2 = bf16[2,16,32,3456]{3,2,0,1:T(8,128)(2,1)} async-done(((bf16[2,16,32,3456]{3,2,0,1:T(8,128)(2,1)}), bf16[2,16,32,3456]{3,2,0,1:T(8,128)(2,1)}, u32[]{:S(2)}, u32[]{:S(2)}) %all-to-all-start.2) | async-done | bytes 7077920 | tf_op jit(solution)/shard_map/all_to_all | solution.py:131
  449.9 9.7 %copy.23 = bf16[2,16,32,3456]{3,1,2,0:T(8,128)(2,1)} copy(bf16[2,16,32,3456]{3,2,0,1:T(8,128)(2,1)} %all-to-all-done.2) | data formatting | bytes 14155776 | tf_op jit(solution)/shard_map/all_to_all | solution.py:131
  459.6 25.5 %reshape.241 = bf16[2,16,32,48,72,1]{4,3,1,2,0,5:T(8,128)(2,1)} reshape(bf16[2,16,32,3456]{3,1,2,0:T(8,128)(2,1)} %copy.23) | data formatting | bytes 14155776 | tf_op jit(solution)/shard_map/reshape | solution.py:101
  485.1 24.6 %bitcast_convert_fusion.1 = bf16[8,64,2,32,72]{4,1,3,2,0:T(8,128)(2,1)} fusion(bf16[2,16,32,48,72,1]{4,3,1,2,0,5:T(8,128)(2,1)} %reshape.241, f32[8,64]{1,0:T(8,128)S(1)} %fusion.102, f32[16,48]{1,0:T(8,128)S(1)} %multiply_add_fusion, f32[8,64]{1,0:T(8,128)S(1)} %fusion.93, pred[8,64]{1,0:T(8,128)(4,1)S(1)} %fusion.90), kind=kOutput, calls=%fused_computation.5 | convolution fusion | flops 3628204032 | bytes 11804160 | tf_op jit(solution)/shard_map/fbaiz,bick->fczak/dot_general | solution.py:102
  509.7 10.7 %copy.24 = bf16[2,8,72,2048]{3,2,0,1:T(8,128)(2,1)} copy(bf16[2,8,72,2048]{2,3,0,1:T(8,128)(2,1)} %bitcast.99) | data formatting | bytes 9437184 | tf_op jit(solution)/shard_map/reshape | solution.py:103
  525.3 55.8 %all-to-all-done.3 = bf16[2,8,72,2048]{3,2,0,1:T(8,128)(2,1)} async-done(((bf16[2,8,72,2048]{3,2,0,1:T(8,128)(2,1)}), bf16[2,8,72,2048]{3,2,0,1:T(8,128)(2,1)}, u32[]{:S(2)}, u32[]{:S(2)}) %all-to-all-start.3) | async-done | bytes 4718624 | tf_op jit(solution)/shard_map/all_to_all | solution.py:134
  581.1 11.6 %copy.25 = bf16[2,8,72,2048]{2,1,3,0:T(8,128)(2,1)} copy(bf16[2,8,72,2048]{3,2,0,1:T(8,128)(2,1)} %all-to-all-done.3) | data formatting | bytes 9437184 | tf_op jit(solution)/shard_map/all_to_all | solution.py:134
  592.7 13.1 %reshape.232 = bf16[2,576,32,64]{1,3,2,0:T(8,128)(2,1)} reshape(bf16[2,8,72,2048]{2,1,3,0:T(8,128)(2,1)} %copy.25) | data formatting | bytes 9437184 | tf_op jit(solution)/shard_map/reshape | solution.py:108
  605.8 8.6 %fusion.76 = f32[2,32,64,384]{3,2,1,0:T(8,128)S(1)} fusion(bf16[2,576,32,64]{1,3,2,0:T(8,128)(2,1)} %reshape.232, f32[384]{0:T(512)S(1)} %fusion.113, f32[576]{0:T(1024)S(1)} %add_multiply_fusion.3), kind=kOutput, calls=%fused_computation.90 | convolution fusion | flops 1812824064 | bytes 11013888 | tf_op jit(solution)/shard_map/fzak,zn->fakn/dot_general | solution.py:109
  (36 shorter events, 38.3 us)
Async XLA Ops:
  0.6 613.8 %copy-start = (bf16[384,384]{1,0:T(8,128)(2,1)S(1)}, bf16[384,384]{1,0:T(8,128)(2,1)}, u32[]{:S(2)}) copy-start(bf16[384,384]{1,0:T(8,128)(2,1)} %param.10) | copy-start | bytes 884740
  41.2 60.5 %all-to-all-start = ((bf16[2,8,72,2048]{3,2,0,1:T(8,128)(2,1)}), bf16[2,8,72,2048]{3,2,0,1:T(8,128)(2,1)}, u32[]{:S(2)}, u32[]{:S(2)}) async-start(bf16[2,8,72,2048]{3,2,0,1:T(8,128)(2,1)} %copy.17), calls=%async_computation | async-start | bytes 9437184 | tf_op jit(solution)/shard_map/all_to_all | solution.py:125
  174.7 7.1 %copy-start.3 = (f32[72]{0:T(128)S(1)}, f32[72]{0:T(128)}, u32[]{:S(2)}) copy-start(f32[72]{0:T(128)} %param.8) | copy-start | bytes 868
  174.7 113.8 %all-to-all-start.1 = ((bf16[2,16,32,3456]{3,2,0,1:T(8,128)(2,1)}), bf16[2,16,32,3456]{3,2,0,1:T(8,128)(2,1)}, u32[]{:S(2)}, u32[]{:S(2)}) async-start(bf16[2,16,32,3456]{3,2,0,1:T(8,128)(2,1)} %reshape.227), calls=%async_computation.1 | async-start | bytes 14155776 | tf_op jit(solution)/shard_map/all_to_all | solution.py:128
  335.9 113.9 %all-to-all-start.2 = ((bf16[2,16,32,3456]{3,2,0,1:T(8,128)(2,1)}), bf16[2,16,32,3456]{3,2,0,1:T(8,128)(2,1)}, u32[]{:S(2)}, u32[]{:S(2)}) async-start(bf16[2,16,32,3456]{3,2,0,1:T(8,128)(2,1)} %copy.22), calls=%async_computation.2 | async-start | bytes 14155776 | tf_op jit(solution)/shard_map/all_to_all | solution.py:131
  520.3 60.8 %all-to-all-start.3 = ((bf16[2,8,72,2048]{3,2,0,1:T(8,128)(2,1)}), bf16[2,8,72,2048]{3,2,0,1:T(8,128)(2,1)}, u32[]{:S(2)}, u32[]{:S(2)}) async-start(bf16[2,8,72,2048]{3,2,0,1:T(8,128)(2,1)} %copy.24), calls=%async_computation.3 | async-start | bytes 9437184 | tf_op jit(solution)/shard_map/all_to_all | solution.py:134
  605.8 8.6 %copy-start.1 = (bf16[32,64,384]{2,1,0:T(8,128)(2,1)S(1)}, bf16[32,64,384]{2,1,0:T(8,128)(2,1)}, u32[]{:S(2)}) copy-start(bf16[32,64,384]{2,1,0:T(8,128)(2,1)} %param.6) | copy-start | bytes 4718596
  614.4 1.4 copy-start.2
  615.9 1.2 copy-start.4
  615.9 1.2 copy-start.5
where the time goes:
time: 634 us; the launch traced here: 623 us
  waiting for transfers between devices  324 us (51%)
  local copies, waits for them, and re-layouts  153 us (24%)
  matrix products  106 us (17%)
  starting transfers between devices  24.5 us (4%)
  other arithmetic  14.4 us (2%)
    all_to_all x1, waiting for transfers between devices, per_device(): lax.all_to_all(fold_x(fluxes, back_x, row_count), 'row', split_axis=1, co...  107 us
    all_to_all x1, waiting for transfers between devices, per_device(): lax.all_to_all(spread, 'row', split_axis=1, concat_axis=2, tiled=True)  107 us
    all_to_all x1, waiting for transfers between devices, per_device(): lax.all_to_all(fold_y(folded, back_y, span_y, depth_part, col_count), 'co...  55.8 us
    all_to_all x1, waiting for transfers between devices, per_device(): lax.all_to_all(lifted, 'col', split_axis=1, concat_axis=3, tiled=True)  55 us
    reshape x2, local copies, waits for them, and re-layouts, spread_rows(): parts = arrived.reshape(fields, depth_part, col_count, modes_x, modes_y)  29.4 us
    reshape x1, local copies, waits for them, and re-layouts, fold_y(): parts = arrived.reshape(fields, row_count, modes_x, span_y, depth_part)  25.5 us
    dot_general x1, matrix products, fold_y(): jnp.einsum('fbaiz,bick->fczak', parts, back_y, preferred_element_type=jnp...  24.6 us
    dot_general x1, matrix products, spread_rows(): jnp.einsum('fzcak,ckbi->fbaiz', parts, along_y, preferred_element_type=jn...  23.5 us
  transfers between devices with their start and end apart: 4, of which 4 were waited for; matrix products, arithmetic and copies ran while one was open for 0% of the time, Pallas kernels for 0%

commit v1 on v0

v1 whole, which is shorter than its diff:
```python
import functools
import math

import jax
import jax.numpy as jnp
import numpy as np
from jax import lax
from jax.experimental import pallas as pl
from jax.experimental.pallas import tpu as pltpu
from jax.sharding import PartitionSpec as P

KX = 512
KY = 512
NZ = 384
XG = 768
YG = 768
ZG = 576

explicit_step = 0.5
diffuse_buoy = 0.5
diffuse_vel = 0.25
couple_buoy = 0.7
couple_vel = 0.7

ROWS = 16
COLS = 8
A = KX // ROWS
K = KY // COLS
PAIRS = A // 2
LANES = 2 * K
G = 3
ZPART = ZG // COLS
ZC = ZPART // G
ZI = 3
YH = YG // 2
BF = jnp.bfloat16
F32 = jnp.float32
MESH = pl.DeviceIdType.MESH
VMEM_LIMIT = 66_500_000


def trig(modes, points):
    order = np.arange(modes)
    freq = ((order + 1) // 2).astype(np.float32)
    step = np.float32(2.0 * math.pi / points)
    angle = (step * freq)[:, None] * np.arange(points, dtype=np.float32)[None, :]
    angle = angle.astype(np.float64)
    values = np.where((order % 2 == 0)[:, None], np.cos(angle), np.sin(angle))
    return order, values.astype(np.float32)


def fourier_eval(modes, points):
    _, values = trig(modes, points)
    return (values * np.float32(math.sqrt(2.0 / modes))).astype(BF)


def fourier_proj(modes, points):
    order, values = trig(modes, points)
    weight = np.where(order == 0, 1.0 / points, 2.0 / points).astype(np.float32)
    return (values * weight[:, None] * np.float32(math.sqrt(modes / 2.0))).T.astype(BF)


def cheb_tables(degree, points):
    order = np.arange(degree, dtype=np.float32)
    theta = np.float32(math.pi) * (np.arange(points, dtype=np.float32) + np.float32(0.5))
    theta = theta / np.float32(points)
    angle = (order[:, None] * theta[None, :]).astype(np.float64)
    cos, sin = np.cos(angle).astype(np.float32), np.sin(angle).astype(np.float32)
    norm = np.float32(math.sqrt(2.0 / degree))
    weight = np.where(order == 0, 1.0 / points, 2.0 / points).astype(np.float32)
    levels = cos * norm
    slopes = -(order[:, None] / np.float32(degree)) * sin * norm
    projector = (cos * weight[:, None] * np.float32(math.sqrt(degree / 2.0))).T
    return levels.astype(BF), slopes.astype(BF), projector.astype(BF)


def tables():
    levels, slopes, projector = cheb_tables(NZ, ZG)

    def by_chunk(rows):
        parts = np.asarray(rows).reshape(COLS, G, ZC, NZ).transpose(1, 0, 2, 3)
        return np.ascontiguousarray(parts)

    lift = by_chunk(levels.T).reshape(G, COLS * ZC, NZ)
    slope = by_chunk(slopes.T).reshape(G, COLS * ZC, NZ)
    drop = by_chunk(projector).reshape(ZG, NZ)
    place = np.arange(KX).reshape(ROWS, PAIRS, 2).transpose(0, 2, 1).reshape(-1)
    eval_y = np.asarray(fourier_eval(KY, YG))
    proj_y = np.asarray(fourier_proj(KY, YG))
    eval_x = np.ascontiguousarray(np.asarray(fourier_eval(KX, XG)).T[:, place])
    proj_x = np.ascontiguousarray(np.asarray(fourier_proj(KX, XG)).T[place, :])
    return lift, slope, drop, eval_y, proj_y, eval_x, proj_x


def mm(left, right, dims=((1,), (0,))):
    return lax.dot_general(left, right, (dims, ((), ())), preferred_element_type=F32)


def kernel(
    vel, buoy, lift, slope, drop, eval_y, proj_y, eval_x, proj_x, strata, eig_val, eig_left, eig_right,
    out_buoy, out_vel,
    lifted, arrived, spread, grid, returned, folded, tall, wide_eval, wide_proj, flux, strata_all,
    colf_s, colf_r, rowf_s, rowf_r, rowb_s, rowb_r, colb_s, colb_r, strat_s, strat_r,
):
    row, col = lax.axis_index("row"), lax.axis_index("col")
    high = row // (ROWS // 2)
    base, low = (col // 2) * 2, col % 2
    part = base + (low + high) % 2

    def col_of(q):
        return (row, (q // 2) * 2 + (q % 2 + high) % 2)

    def row_of(t):
        return (t, base + (low + high + t // (ROWS // 2)) % 2)

    barrier = pltpu.get_barrier_semaphore()

    @pl.loop(1, COLS)
    def _(i):
        pl.semaphore_signal(barrier, inc=1, device_id=col_of((part + i) % COLS), device_id_type=MESH)

    @pl.loop(1, ROWS)
    def _(i):
        pl.semaphore_signal(barrier, inc=1, device_id=row_of((row + i) % ROWS), device_id_type=MESH)

    pl.semaphore_wait(barrier, COLS + ROWS - 2)

    def remote(src, dst, send, recv, device):
        return pltpu.make_async_remote_copy(
            src_ref=src, dst_ref=dst, send_sem=send, recv_sem=recv, device_id=device, device_id_type=MESH
        )

    swap = remote(strata, strata_all.at[1], strat_s, strat_r, (row, base + 1 - low))
    swap.start()
    strata_all[0] = strata[...]

    def col_fwd(g, q):
        return remote(lifted.at[g, q], arrived.at[g, col], colf_s.at[g, q], colf_r.at[g, col], col_of(q))

    def col_fwd_in(g, s):
        block = arrived.at[g, s]
        return remote(block, block, colf_s.at[g, s], colf_r.at[g, s], col_of(0))

    def col_fwd_own(g):
        return pltpu.make_async_copy(lifted.at[g, part], arrived.at[g, col], colf_r.at[g, col])

    def row_fwd(g, t):
        mine = pl.ds(pl.multiple_of(row * A, A), A)
        return remote(spread.at[g, t], grid.at[g, :, :, mine, :], rowf_s.at[g, t], rowf_r.at[g, row], row_of(t))

    def row_fwd_in(g, t):
        block = grid.at[g, :, :, pl.ds(pl.multiple_of(t * A, A), A), :]
        return remote(block, block, rowf_s.at[g, t], rowf_r.at[g, t], row_of(t))

    def row_fwd_own(g):
        mine = pl.ds(pl.multiple_of(row * A, A), A)
        return pltpu.make_async_copy(spread.at[g, row], grid.at[g, :, :, mine, :], rowf_r.at[g, row])

    def row_back(g, t):
        theirs = pl.ds(pl.multiple_of(t * A, A), A)
        return remote(grid.at[g, :, :, theirs, :], returned.at[g, row], rowb_s.at[g, t], rowb_r.at[g, row], row_of(t))

    def row_back_in(g, t):
        block = returned.at[g, t]
        return remote(block, block, rowb_s.at[g, t], rowb_r.at[g, t], row_of(t))

    def row_back_own(g):
        mine = pl.ds(pl.multiple_of(row * A, A), A)
        return pltpu.make_async_copy(grid.at[g, :, :, mine, :], returned.at[g, row], rowb_r.at[g, row])

    def col_back(g, s):
        return remote(arrived.at[g, s], folded.at[g, part], colb_s.at[g, s], colb_r.at[g, part], (row, s))

    def col_back_in(g, q):
        block = folded.at[g, q]
        return remote(block, block, colb_s.at[g, q], colb_r.at[g, q], col_of(q))

    def col_back_own(g):
        return pltpu.make_async_copy(arrived.at[g, col], folded.at[g, part], colb_r.at[g, part])

    def others(first, count, do):
        @pl.loop(1, count)
        def _(i):
            do((first + i) % count)

    half = COLS * ZC * PAIRS

    @pl.loop(0, G)
    def _(g):
        @pl.loop(0, PAIRS)
        def _(p):
            rows = pl.ds(pl.multiple_of(p * LANES, LANES), LANES)
            tall[pl.ds(p, COLS * ZC, stride=PAIRS), :] = mm(lift[g], vel[rows, :], ((1,), (1,)))
            tall[pl.ds(half + p, COLS * ZC, stride=PAIRS), :] = mm(slope[g], buoy[rows, :], ((1,), (1,)))

        size = ZC * PAIRS

        @pl.loop(0, COLS)
        def _(q):
            for f in range(2):
                rows = pl.ds(pl.multiple_of(q * size + f * half, size), size)
                lifted[g, q, f] = tall[rows, :].astype(BF)

        others(part, COLS, lambda q: col_fwd(g, q).start())
        col_fwd_own(g).start()

    @pl.loop(0, COLS)
    def _(s):
        for a in range(2):
            for h in range(2):
                own = pl.ds(pl.multiple_of(s * LANES + a * K, K), K)
                other = pl.ds(pl.multiple_of(s * LANES + (1 - a) * K, K), K)
                wide_eval[a * 2 + h, own, :] = eval_y[pl.ds(pl.multiple_of(s * K, K), K), h * YH : (h + 1) * YH]
                wide_eval[a * 2 + h, other, :] = jnp.zeros((K, YH), BF)

    @pl.loop(0, G)
    def _(g):
        others(col, COLS, lambda s: col_fwd_in(g, s).wait_recv())
        col_fwd_own(g).wait()

        @pl.loop(0, 2)
        def _(f):
            left = jnp.concatenate([arrived[g, s, f] for s in range(COLS)], axis=1)
            for a in range(2):
                for h in range(2):
                    values = mm(left, wide_eval[a * 2 + h]).astype(BF)
                    spread[g, h * 8 : (h + 1) * 8, f, :, a * PAIRS : (a + 1) * PAIRS, :] = values.reshape(
                        8, ZI, PAIRS, YH
                    )

        others(row, ROWS, lambda t: row_fwd(g, t).start())
        row_fwd_own(g).start()

    lane = lax.broadcasted_iota(jnp.int32, (YG, LANES), 1)
    for j in range(COLS // 2):
        tile = proj_y[:, j * LANES : (j + 1) * LANES].astype(F32)
        turned = pltpu.roll(tile, K, 1)
        for s in (2 * j, 2 * j + 1):
            straight, moved = (tile, turned) if s % 2 == 0 else (turned, tile)
            for a in range(2):
                keep = jnp.where((lane < K) == (a == 0), straight if a == 0 else moved, 0.0).astype(BF)
                wide_proj[s // 4, a * YG : (a + 1) * YG, (s % 4) * LANES : (s % 4 + 1) * LANES] = keep

    swap.wait()

    @pl.loop(0, G)
    def _(g):
        others(row, ROWS, lambda t: row_fwd_in(g, t).wait_recv())
        row_fwd_own(g).wait()

        @pl.loop(0, ZI)
        def _(i):
            level = strata_all[high, pl.ds(g * ZC + (row % 8) * ZI + i, 1), :]
            tile = XG // 3
            for x in range(3):
                rows = slice(x * tile, (x + 1) * tile)
                velocity = mm(eval_x[rows, :], grid[g, 0, i]).astype(BF).astype(F32)
                gradient = mm(eval_x[rows, :], grid[g, 1, i]).astype(BF).astype(F32)
                flux[0, rows, :] = (-(velocity * gradient) - level * velocity).astype(BF)
                flux[1, rows, :] = (-(velocity * jnp.abs(velocity))).astype(BF)
            for f in range(2):
                grid[g, f, i] = mm(proj_x[...], flux[f]).astype(BF)

        others(row, ROWS, lambda t: row_back(g, t).start())
        row_back_own(g).start()

    @pl.loop(0, G)
    def _(g):
        others(row, ROWS, lambda t: row_back_in(g, t).wait_recv())
        row_back_own(g).wait()

        @pl.loop(0, 2)
        def _(f):
            left = jnp.concatenate(
                [
                    returned[g, h * 8 : (h + 1) * 8, f, :, a * PAIRS : (a + 1) * PAIRS, :].reshape(ZC * PAIRS, YH)
                    for a in range(2)
                    for h in range(2)
                ],
                axis=1,
            )
            for h in range(2):
                values = mm(left, wide_proj[h]).astype(BF)
                for s in range(4):
                    arrived[g, 4 * h + s, f] = values[:, s * LANES : (s + 1) * LANES]

        others(col, COLS, lambda s: col_back(g, s).start())
        col_back_own(g).start()

    for g in range(G):
        others(part, COLS, lambda q: col_back_in(g, q).wait_recv())
        col_back_own(g).wait()

    for f, (field, out) in enumerate(((buoy, out_buoy), (vel, out_vel))):
        size = ZC * PAIRS

        @pl.loop(0, G * COLS)
        def _(i):
            tall[pl.ds(pl.multiple_of(i * size, size), size), :] = folded[i // COLS, i % COLS, f].astype(F32)

        @pl.loop(0, PAIRS)
        def _(p):
            rows = pl.ds(pl.multiple_of(p * LANES, LANES), LANES)
            column = tall[pl.ds(p, ZG, stride=PAIRS), :].astype(BF)
            tend = mm(column, drop[...], ((0,), (0,)))
            out[rows, :] = (field[rows, :].astype(F32) + explicit_step * tend).astype(BF)

    block = 256

    @pl.loop(0, A * K // block)
    def _(i):
        rows = pl.ds(pl.multiple_of(i * block, block), block)
        modal_buoy = mm(out_buoy[rows, :], eig_left[...])
        modal_vel = mm(out_vel[rows, :], eig_left[...])
        place = i * block + lax.broadcasted_iota(jnp.int32, (block, NZ), 0)
        freq_x = ((row * A + place // K + 1) // 2).astype(F32) * (2.0 / KX)
        freq_y = ((col * K + place % K + 1) // 2).astype(F32) * (2.0 / KY)
        lapl = 4.0 * (freq_x * freq_x + freq_y * freq_y) + eig_val[...]
        diag_buoy = 1.0 + diffuse_buoy * lapl
        diag_vel = 1.0 + diffuse_vel * lapl
        inverse = 1.0 / (diag_buoy * diag_vel + couple_buoy * couple_vel)
        solved_buoy = ((diag_vel * modal_buoy - couple_buoy * modal_vel) * inverse).astype(BF)
        solved_vel = ((diag_buoy * modal_vel + couple_vel * modal_buoy) * inverse).astype(BF)
        out_buoy[rows, :] = mm(solved_buoy, eig_right[...]).astype(BF)
        out_vel[rows, :] = mm(solved_vel, eig_right[...]).astype(BF)

    @pl.loop(0, G)
    def _(g):
        others(part, COLS, lambda q: col_fwd(g, q).wait_send())
        others(row, ROWS, lambda t: row_fwd(g, t).wait_send())
        others(row, ROWS, lambda t: row_back(g, t).wait_send())
        others(col, COLS, lambda s: col_back(g, s).wait_send())


def per_device(buoy, vel_w, strat, eig_val, eig_left, eig_right):
    modes = A * K
    dma = pltpu.SemaphoreType.DMA
    strata = jnp.broadcast_to(strat[:, None], (ZPART, YH))
    vmem = pl.BlockSpec(memory_space=pltpu.VMEM)
    shape = jax.ShapeDtypeStruct((modes, NZ), BF)
    size = ZC * PAIRS
    consts = [jnp.asarray(t) for t in tables()]
    new_buoy, new_vel = pl.pallas_call(
        kernel,
        out_shape=(shape, shape),
        in_specs=[vmem] * 13,
        out_specs=(vmem, vmem),
        scratch_shapes=[
            pltpu.VMEM((G, COLS, 2, size, LANES), BF),
            pltpu.VMEM((G, COLS, 2, size, LANES), BF),
            pltpu.VMEM((G, ROWS, 2, ZI, A, YH), BF),
            pltpu.VMEM((G, 2, ZI, KX, YH), BF),
            pltpu.VMEM((G, ROWS, 2, ZI, A, YH), BF),
            pltpu.VMEM((G, COLS, 2, size, LANES), BF),
            pltpu.VMEM((ZG * PAIRS, LANES), F32),
            pltpu.VMEM((4, COLS * LANES, YH), BF),
            pltpu.VMEM((2, 2 * YG, COLS * LANES // 2), BF),
            pltpu.VMEM((2, XG, YH), BF),
            pltpu.VMEM((2, ZPART, YH), F32),
            dma((G, COLS)), dma((G, COLS)), dma((G, ROWS)), dma((G, ROWS)),
            dma((G, ROWS)), dma((G, ROWS)), dma((G, COLS)), dma((G, COLS)),
            dma, dma,
        ],
        compiler_params=pltpu.CompilerParams(
            collective_id=0, has_side_effects=True, vmem_limit_bytes=VMEM_LIMIT
        ),
        name="section",
    )(
        vel_w.reshape(modes, NZ), buoy.reshape(modes, NZ), *consts, strata,
        eig_val.reshape(1, NZ), eig_left, eig_right,
    )
    return new_buoy.reshape(buoy.shape), new_vel.reshape(buoy.shape)


def solution(mesh):
    in_specs = (P("row", "col", None), P("row", "col", None), P("col"), P(), P(), P())
    out_specs = (P("row", "col", None), P("row", "col", None))
    return jax.shard_map(
        per_device, mesh=mesh, in_specs=in_specs, out_specs=out_specs, check_vma=False
    )
```

time: 634 us -> 272 us (0.43)
  the two profiles are of different devices: /device:TPU:100 before, /device:TPU:97 now
where the time goes in v1:
time: 272 us
  Pallas kernels  265 us (97%)
  local copies, waits for them, and re-layouts  6.6 us (2%)
    pallas_call x1, Pallas kernels, per_device(): pl.pallas_call(kernel, out_shape=(shape, shape), in_specs=[vmem] * 13, ou...  265 us

profile of v1, /device:TPU:97, one launch (start us, length us, event | category | flops | bytes accessed | tf_op | source)
XLA Modules:
  0.0 272.2 jit_solution(12780931417706734187)
XLA Ops:
  0.6 1.2 reshape.22.eig_val
  1.9 1.4 broadcast_in_dim.2.strata
  3.3 265.0 %section.1 = (bf16[2048,384]{1,0:T(8,128)(2,1)}, bf16[2048,384]{1,0:T(8,128)(2,1)}) custom-call(bf16[2048,384]{1,0:T(8,128)(2,1)} %bitcast.4, bf16[2048,384]{1,0:T(8,128)(2,1)} %bitcast.5, bf16[3,192,384]{2,1,0:T(8,128)(2,1)} %constant.14.clone.lift, bf16[3,192,384]{2,1,0:T(8,128)(2,1)} %constant.15.clone.slope, bf16[576,384]{1,0:T(8,128)(2,1)} %constant.16.clone.drop, ...), custom_call_target="tpu_custom_call" | custom-call | tf_op jit(solution)/shard_map/section/pallas_call | solution.py:343
  268.3 0.0 copy-start
  268.3 2.8 %copy.17 = bf16[32,64,384]{2,1,0:T(8,128)(2,1)} copy(bf16[32,64,384]{2,1,0:T(8,128)(2,1)} %bitcast.7) | data formatting | bytes 3145728
  271.1 0.0 copy-done
  271.1 1.1 copy.18
Async XLA Ops:
  268.3 2.8 %copy-start = (bf16[2048,384]{1,0:T(8,128)(2,1)S(1)}, bf16[2048,384]{1,0:T(8,128)(2,1)}, u32[]{:S(2)}) copy-start(bf16[2048,384]{1,0:T(8,128)(2,1)} %get-tuple-element.5) | copy-start | bytes 4718596

commit v2 on v1

v2 whole, which is shorter than its diff:
```python
import functools
import math

import jax
import jax.numpy as jnp
import numpy as np
from jax import lax
from jax.experimental import pallas as pl
from jax.experimental.pallas import tpu as pltpu
from jax.sharding import PartitionSpec as P

KX = 512
KY = 512
NZ = 384
XG = 768
YG = 768
ZG = 576

explicit_step = 0.5
diffuse_buoy = 0.5
diffuse_vel = 0.25
couple_buoy = 0.7
couple_vel = 0.7

ROWS = 16
COLS = 8
A = KX // ROWS
K = KY // COLS
PAIRS = A // 2
LANES = 2 * K
G = 9
ZPART = ZG // COLS
ZC = ZPART // G
SIZE = ZC * PAIRS
YH = YG // 2
TWO = 2 * LANES
TALL = ZG * PAIRS // 2
ENDS = (4, 7, 9)
BF = jnp.bfloat16
F32 = jnp.float32
MESH = pl.DeviceIdType.MESH
VMEM_LIMIT = 67_000_000


def trig(modes, points):
    order = np.arange(modes)
    freq = ((order + 1) // 2).astype(np.float32)
    step = np.float32(2.0 * math.pi / points)
    angle = (step * freq)[:, None] * np.arange(points, dtype=np.float32)[None, :]
    angle = angle.astype(np.float64)
    values = np.where((order % 2 == 0)[:, None], np.cos(angle), np.sin(angle))
    return order, values.astype(np.float32)


def fourier_eval(modes, points):
    _, values = trig(modes, points)
    return (values * np.float32(math.sqrt(2.0 / modes))).astype(BF)


def fourier_proj(modes, points):
    order, values = trig(modes, points)
    weight = np.where(order == 0, 1.0 / points, 2.0 / points).astype(np.float32)
    return (values * weight[:, None] * np.float32(math.sqrt(modes / 2.0))).T.astype(BF)


def cheb_tables(degree, points):
    order = np.arange(degree, dtype=np.float32)
    theta = np.float32(math.pi) * (np.arange(points, dtype=np.float32) + np.float32(0.5))
    theta = theta / np.float32(points)
    angle = (order[:, None] * theta[None, :]).astype(np.float64)
    cos, sin = np.cos(angle).astype(np.float32), np.sin(angle).astype(np.float32)
    norm = np.float32(math.sqrt(2.0 / degree))
    weight = np.where(order == 0, 1.0 / points, 2.0 / points).astype(np.float32)
    levels = cos * norm
    slopes = -(order[:, None] / np.float32(degree)) * sin * norm
    projector = (cos * weight[:, None] * np.float32(math.sqrt(degree / 2.0))).T
    return levels.astype(BF), slopes.astype(BF), projector.astype(BF)


def tables():
    levels, slopes, projector = cheb_tables(NZ, ZG)
    drop = np.asarray(projector).reshape(COLS, G, ZC, NZ).transpose(1, 0, 2, 3).reshape(ZG, NZ)
    lift, slope = (np.ascontiguousarray(np.asarray(t).T) for t in (levels, slopes))
    return lift, slope, np.ascontiguousarray(drop), fourier_eval(KY, YG), np.ascontiguousarray(fourier_proj(KY, YG))


def mm(left, right, dims=((1,), (0,))):
    return lax.dot_general(left, right, (dims, ((), ())), preferred_element_type=F32)


def kernel(
    vel, buoy, lift, slope, drop, evals, projs, strat, eig_val, eig_left, eig_right,
    out_buoy, out_vel,
    lifted, arrived, spread, grid, returned, folded, tall, wide_eval, wide_proj, eval_x, proj_x, flux, partial,
    strat_in,
    colf_s, colf_r, rowf_s, rowf_r, rowb_s, rowb_r, colb_s, colb_r, strat_s, strat_r,
):
    row, col = lax.axis_index("row"), lax.axis_index("col")
    high = row // (ROWS // 2)
    base, low = (col // 2) * 2, col % 2
    part = base + (low + high) % 2

    def col_of(q):
        return (row, (q // 2) * 2 + (q % 2 + high) % 2)

    def row_of(t):
        return (t, base + (low + high + t // (ROWS // 2)) % 2)

    barrier = pltpu.get_barrier_semaphore()

    @pl.loop(1, COLS)
    def _(i):
        pl.semaphore_signal(barrier, inc=1, device_id=col_of((part + i) % COLS), device_id_type=MESH)

    @pl.loop(1, ROWS)
    def _(i):
        pl.semaphore_signal(barrier, inc=1, device_id=row_of((row + i) % ROWS), device_id_type=MESH)

    pl.semaphore_wait(barrier, COLS + ROWS - 2)

    def remote(src, dst, send, recv, device):
        return pltpu.make_async_remote_copy(
            src_ref=src, dst_ref=dst, send_sem=send, recv_sem=recv, device_id=device, device_id_type=MESH
        )

    swap = remote(strat, strat_in, strat_s, strat_r, (row, base + 1 - low))
    swap.start()

    def col_fwd(g, q):
        return remote(lifted.at[g, q], arrived.at[g, col], colf_s.at[g, q], colf_r.at[g, col], col_of(q))

    def col_fwd_in(g, s):
        block = arrived.at[g, s]
        return remote(block, block, colf_s.at[g, s], colf_r.at[g, s], col_of(0))

    def col_fwd_own(g):
        return pltpu.make_async_copy(lifted.at[g, part], arrived.at[g, col], colf_r.at[g, col])

    def row_fwd(g, t):
        mine = pl.ds(pl.multiple_of(row * A, A), A)
        return remote(spread.at[g, t], grid.at[g, :, mine, :], rowf_s.at[g, t], rowf_r.at[g, row], row_of(t))

    def row_fwd_in(g, t):
        block = grid.at[g, :, pl.ds(pl.multiple_of(t * A, A), A), :]
        return remote(block, block, rowf_s.at[g, t], rowf_r.at[g, t], row_of(t))

    def row_fwd_own(g):
        mine = pl.ds(pl.multiple_of(row * A, A), A)
        return pltpu.make_async_copy(spread.at[g, row], grid.at[g, :, mine, :], rowf_r.at[g, row])

    def row_back(g, t):
        theirs = pl.ds(pl.multiple_of(t * A, A), A)
        return remote(grid.at[g, :, theirs, :], returned.at[g, row], rowb_s.at[g, t], rowb_r.at[g, row], row_of(t))

    def row_back_in(g, t):
        block = returned.at[g, t]
        return remote(block, block, rowb_s.at[g, t], rowb_r.at[g, t], row_of(t))

    def row_back_own(g):
        mine = pl.ds(pl.multiple_of(row * A, A), A)
        return pltpu.make_async_copy(grid.at[g, :, mine, :], returned.at[g, row], rowb_r.at[g, row])

    def col_back(g, s):
        return remote(arrived.at[g, s], folded.at[g, part], colb_s.at[g, s], colb_r.at[g, part], (row, s))

    def col_back_in(g, q):
        block = folded.at[g, q]
        return remote(block, block, colb_s.at[g, q], colb_r.at[g, q], col_of(q))

    def col_back_own(g):
        return pltpu.make_async_copy(arrived.at[g, col], folded.at[g, part], colb_r.at[g, part])

    def others(first, count, do):
        @pl.loop(1, count)
        def _(i):
            do((first + i) % count)

    @pl.loop(0, 2)
    def _(side):
        count = ZG // 2
        points = pl.ds(pl.multiple_of(side * count, count), count)
        for f, (table, field) in enumerate(((lift, vel), (slope, buoy))):

            @pl.loop(0, PAIRS // 2)
            def _(p):
                rows = pl.ds(pl.multiple_of(p * TWO, TWO), TWO)
                values = mm(table[points, :], field[rows, :], ((1,), (1,)))
                tall[pl.ds(2 * p, count, stride=PAIRS), :] = values[:, :LANES]
                tall[pl.ds(2 * p + 1, count, stride=PAIRS), :] = values[:, LANES:]

            @pl.loop(0, COLS // 2 * G)
            def _(i):
                rows = pl.ds(pl.multiple_of(i * SIZE, SIZE), SIZE)
                lifted[i % G, side * (COLS // 2) + i // G, f] = tall[rows, :].astype(BF)

    @pl.loop(0, G)
    def _(g):
        others(part, COLS, lambda q: col_fwd(g, q).start())
        col_fwd_own(g).start()

    @pl.loop(0, COLS)
    def _(s):
        for a in range(2):
            own = pl.ds(pl.multiple_of(s * LANES + a * K, K), K)
            other = pl.ds(pl.multiple_of(s * LANES + (1 - a) * K, K), K)
            wide_eval[a, own, :] = evals[pl.ds(pl.multiple_of(s * K, K), K), :]
            wide_eval[a, other, :] = jnp.zeros((K, YG), BF)

    @pl.loop(0, G)
    def _(g):
        others(col, COLS, lambda s: col_fwd_in(g, s).wait_recv())
        col_fwd_own(g).wait()
        left = jnp.concatenate(
            [jnp.concatenate([arrived[g, s, f] for s in range(COLS)], axis=1) for f in range(2)], axis=0
        )
        for a in range(2):
            values = mm(left, wide_eval[a]).astype(BF)
            for f in range(2):
                for h in range(2):
                    block = values[f * SIZE : (f + 1) * SIZE, h * YH : (h + 1) * YH]
                    spread[g, h * 8 : (h + 1) * 8, f, a * PAIRS : (a + 1) * PAIRS, :] = block.reshape(8, PAIRS, YH)

        others(row, ROWS, lambda t: row_fwd(g, t).start())
        row_fwd_own(g).start()

    lane = lax.broadcasted_iota(jnp.int32, (YG, LANES), 1)
    for j in range(COLS // 2):
        tile = projs[:, j * LANES : (j + 1) * LANES].astype(F32)
        turned = pltpu.roll(tile, K, 1)
        for s in (2 * j, 2 * j + 1):
            straight, moved = (tile, turned) if s % 2 == 0 else (turned, tile)
            for a in range(2):
                keep = jnp.where((lane < K) == (a == 0), straight if a == 0 else moved, 0.0).astype(BF)
                wide_proj[a * YG : (a + 1) * YG, s * LANES : (s + 1) * LANES] = keep

    @pl.loop(0, XG // LANES)
    def _(j):
        points = pl.ds(pl.multiple_of(j * LANES, LANES), LANES)

        def ordered(values):
            tall[:KX, :] = values
            return jnp.concatenate(
                [tall[pl.ds(r * A + a, PAIRS, stride=2), :] for r in range(ROWS) for a in range(2)], axis=0
            )

        eval_x[points, :] = ordered(evals[:, points].astype(F32)).T.astype(BF)
        proj_x[:, points] = ordered(projs[points, :].astype(F32).T).astype(BF)

    swap.wait()
    strata = jnp.where(high == 0, strat[...], strat_in[...]).reshape(1, ZPART)
    level_of = lax.broadcasted_iota(jnp.int32, (1, ZPART), 1)

    @pl.loop(0, G)
    def _(g):
        others(row, ROWS, lambda t: row_fwd_in(g, t).wait_recv())
        row_fwd_own(g).wait()
        level = jnp.sum(jnp.where(level_of == g * ZC + row % 8, strata, 0.0), axis=1, keepdims=True)
        right = jnp.concatenate([grid[g, 0], grid[g, 1]], axis=1)
        tile = XG // 3
        for x in range(3):
            rows = slice(x * tile, (x + 1) * tile)
            both = mm(eval_x[rows, :], right).astype(BF).astype(F32)
            velocity, gradient = both[:, :YH], both[:, YH:]
            flux[rows, :YH] = (-(velocity * gradient) - level * velocity).astype(BF)
            flux[rows, YH:] = (-(velocity * jnp.abs(velocity))).astype(BF)
        for x in range(2):
            rows = slice(x * KX // 2, (x + 1) * KX // 2)
            both = mm(proj_x[rows, :], flux[...]).astype(BF)
            grid[g, 0, rows, :] = both[:, :YH]
            grid[g, 1, rows, :] = both[:, YH:]

        others(row, ROWS, lambda t: row_back(g, t).start())
        row_back_own(g).start()

    def to_modes(g):
        others(row, ROWS, lambda t: row_back_in(g, t).wait_recv())
        row_back_own(g).wait()

        def side(f, a, h):
            return returned[g, h * 8 : (h + 1) * 8, f, a * PAIRS : (a + 1) * PAIRS, :].reshape(SIZE, YH)

        left = jnp.concatenate(
            [
                jnp.concatenate([side(f, a, h) for a in range(2) for h in range(2)], axis=1)
                for f in range(2)
            ],
            axis=0,
        )
        half = COLS * LANES // 2
        for n in range(2):
            values = mm(left, wide_proj[:, n * half : (n + 1) * half]).astype(BF)
            for f in range(2):
                for s in range(COLS // 2):
                    arrived[g, n * COLS // 2 + s, f] = values[
                        f * SIZE : (f + 1) * SIZE, s * LANES : (s + 1) * LANES
                    ]

        others(col, COLS, lambda s: col_back(g, s).start())
        col_back_own(g).start()

    def gather(first, last, f, start):
        @pl.loop(first, last)
        def _(g):
            for q in range(COLS):
                place = pl.multiple_of(start + ((g - first) * COLS + q) * SIZE, SIZE)
                tall[pl.ds(place, SIZE), :] = folded[g, q, f].astype(F32)

    def tendency(first, last, p, start):
        count = (last - first) * COLS * ZC
        columns = [tall[pl.ds(start + 2 * p + a, count, stride=PAIRS), :].astype(BF) for a in range(2)]
        rows = slice(first * COLS * ZC, last * COLS * ZC)
        return mm(jnp.concatenate(columns, axis=1), drop[rows, :], ((0,), (0,)))

    def wait_modes(first, last):
        @pl.loop(first, last)
        def _(g):
            others(part, COLS, lambda q: col_back_in(g, q).wait_recv())
            col_back_own(g).wait()

    pl.loop(0, ENDS[0] + 1)(to_modes)
    wait_modes(0, ENDS[0])
    for f in range(2):
        gather(0, ENDS[0], f, 0)

        @pl.loop(0, PAIRS // 2)
        def _(p):
            rows = pl.ds(pl.multiple_of(p * TWO, TWO), TWO)
            partial[f, rows, :] = tendency(0, ENDS[0], p, 0)

    pl.loop(ENDS[0] + 1, ENDS[1] + 1)(to_modes)
    wait_modes(ENDS[0], ENDS[1])
    for f in range(2):
        gather(ENDS[0], ENDS[1], f, 0)

        @pl.loop(0, PAIRS // 2)
        def _(p):
            rows = pl.ds(pl.multiple_of(p * TWO, TWO), TWO)
            partial[f, rows, :] += tendency(ENDS[0], ENDS[1], p, 0)

    pl.loop(ENDS[1] + 1, G)(to_modes)
    wait_modes(ENDS[1], G)
    start = (G - ENDS[1]) * COLS * SIZE
    for f in range(2):
        gather(ENDS[1], G, f, f * start)

    @pl.loop(0, PAIRS // 2)
    def _(p):
        rows = pl.ds(pl.multiple_of(p * TWO, TWO), TWO)
        modal = []
        for f, field in enumerate((buoy, vel)):
            tend = partial[f, rows, :] + tendency(ENDS[1], G, p, f * start)
            rhs = (field[rows, :].astype(F32) + explicit_step * tend).astype(BF)
            modal.append(mm(rhs, eig_left[...]))
        modal_buoy, modal_vel = modal
        place = p * TWO + lax.broadcasted_iota(jnp.int32, (TWO, LANES), 0)
        freq_x = ((row * A + (place >> 6) + 1) >> 1).astype(F32) * (2.0 / KX)
        freq_y = ((col * K + (place & (K - 1)) + 1) >> 1).astype(F32) * (2.0 / KY)
        wave = 4.0 * (freq_x * freq_x + freq_y * freq_y)
        lapl = jnp.concatenate([wave] * (NZ // LANES), axis=1) + eig_val[...].reshape(1, NZ)
        diag_buoy = 1.0 + diffuse_buoy * lapl
        diag_vel = 1.0 + diffuse_vel * lapl
        inverse = 1.0 / (diag_buoy * diag_vel + couple_buoy * couple_vel)
        solved_buoy = ((diag_vel * modal_buoy - couple_buoy * modal_vel) * inverse).astype(BF)
        solved_vel = ((diag_buoy * modal_vel + couple_vel * modal_buoy) * inverse).astype(BF)
        out_buoy[rows, :] = mm(solved_buoy, eig_right[...]).astype(BF)
        out_vel[rows, :] = mm(solved_vel, eig_right[...]).astype(BF)

    @pl.loop(0, G)
    def _(g):
        others(part, COLS, lambda q: col_fwd(g, q).wait_send())
        others(row, ROWS, lambda t: row_fwd(g, t).wait_send())
        others(row, ROWS, lambda t: row_back(g, t).wait_send())
        others(col, COLS, lambda s: col_back(g, s).wait_send())


def per_device(buoy, vel_w, strat, eig_val, eig_left, eig_right):
    modes = A * K
    dma = pltpu.SemaphoreType.DMA
    vmem = pl.BlockSpec(memory_space=pltpu.VMEM)
    shape = jax.ShapeDtypeStruct((modes, NZ), BF)
    consts = [jnp.asarray(t) for t in tables()]
    new_buoy, new_vel = pl.pallas_call(
        kernel,
        out_shape=(shape, shape),
        in_specs=[vmem] * 11,
        out_specs=(vmem, vmem),
        scratch_shapes=[
            pltpu.VMEM((G, COLS, 2, SIZE, LANES), BF),
            pltpu.VMEM((G, COLS, 2, SIZE, LANES), BF),
            pltpu.VMEM((G, ROWS, 2, A, YH), BF),
            pltpu.VMEM((G, 2, KX, YH), BF),
            pltpu.VMEM((G, ROWS, 2, A, YH), BF),
            pltpu.VMEM((G, COLS, 2, SIZE, LANES), BF),
            pltpu.VMEM((TALL, LANES), F32),
            pltpu.VMEM((2, COLS * LANES, YG), BF),
            pltpu.VMEM((2 * YG, COLS * LANES), BF),
            pltpu.VMEM((XG, KX), BF),
            pltpu.VMEM((KX, XG), BF),
            pltpu.VMEM((XG, 2 * YH), BF),
            pltpu.VMEM((2, modes, NZ), F32),
            pltpu.VMEM((ZPART,), F32),
            dma((G, COLS)), dma((G, COLS)), dma((G, ROWS)), dma((G, ROWS)),
            dma((G, ROWS)), dma((G, ROWS)), dma((G, COLS)), dma((G, COLS)),
            dma, dma,
        ],
        compiler_params=pltpu.CompilerParams(
            collective_id=0, has_side_effects=True, vmem_limit_bytes=VMEM_LIMIT
        ),
        name="section",
    )(
        vel_w.reshape(modes, NZ), buoy.reshape(modes, NZ), *consts, strat, eig_val, eig_left, eig_right
    )
    return new_buoy.reshape(buoy.shape), new_vel.reshape(buoy.shape)


def solution(mesh):
    in_specs = (P("row", "col", None), P("row", "col", None), P("col"), P(), P(), P())
    out_specs = (P("row", "col", None), P("row", "col", None))
    return jax.shard_map(
        per_device, mesh=mesh, in_specs=in_specs, out_specs=out_specs, check_vma=False
    )
```

time: 272 us -> 224 us (0.82)
  the two profiles are of different devices: /device:TPU:97 before, /device:TPU:5 now
where the time goes in v2:
time: 224 us; the launch traced here: 223 us
  Pallas kernels  218 us (97%)
  local copies, waits for them, and re-layouts  3.98 us (2%)
    pallas_call x1, Pallas kernels, per_device(): pl.pallas_call(kernel, out_shape=(shape, shape), in_specs=[vmem] * 11, ou...  218 us

profile of v2, /device:TPU:5, one launch (start us, length us, event | category | flops | bytes accessed | tf_op | source)
XLA Modules:
  0.0 223.0 jit_solution(10694549032415857111)
XLA Ops:
  0.6 218.3 %section.1 = (bf16[2048,384]{1,0:T(8,128)(2,1)}, bf16[2048,384]{1,0:T(8,128)(2,1)}) custom-call(bf16[2048,384]{1,0:T(8,128)(2,1)} %bitcast.6, bf16[2048,384]{1,0:T(8,128)(2,1)} %bitcast.7, bf16[576,384]{1,0:T(8,128)(2,1)} %constant.10.clone.lift, bf16[576,384]{1,0:T(8,128)(2,1)} %constant.11.clone.slope, bf16[576,384]{1,0:T(8,128)(2,1)} %constant.12.clone.drop, ...), custom_call_target="tpu_custom_call" | custom-call | tf_op jit(solution)/shard_map/section/pallas_call | solution.py:382
  219.0 0.0 copy-start
  219.0 2.8 %copy.15 = bf16[32,64,384]{2,1,0:T(8,128)(2,1)} copy(bf16[32,64,384]{2,1,0:T(8,128)(2,1)} %bitcast.5) | data formatting | bytes 3145728
  221.8 0.0 copy-done
  221.8 1.1 copy.16
Async XLA Ops:
  219.0 2.8 %copy-start = (bf16[2048,384]{1,0:T(8,128)(2,1)S(1)}, bf16[2048,384]{1,0:T(8,128)(2,1)}, u32[]{:S(2)}) copy-start(bf16[2048,384]{1,0:T(8,128)(2,1)} %get-tuple-element.5) | copy-start | bytes 4718596

commit v3 on v2

--- a/solution.py
+++ b/solution.py
@@ -29,13 +29,14 @@
 PAIRS = A // 2
 LANES = 2 * K
 G = 9
+PASSES = 3
 ZPART = ZG // COLS
 ZC = ZPART // G
 SIZE = ZC * PAIRS
 YH = YG // 2
 TWO = 2 * LANES
-TALL = ZG * PAIRS // 2
-ENDS = (4, 7, 9)
+TALL = 5 * COLS * SIZE
+ENDS = (5, 8, 9)
 BF = jnp.bfloat16
 F32 = jnp.float32
 MESH = pl.DeviceIdType.MESH
@@ -80,7 +81,10 @@
 def tables():
     levels, slopes, projector = cheb_tables(NZ, ZG)
     drop = np.asarray(projector).reshape(COLS, G, ZC, NZ).transpose(1, 0, 2, 3).reshape(ZG, NZ)
-    lift, slope = (np.ascontiguousarray(np.asarray(t).T) for t in (levels, slopes))
+    lift, slope = (
+        np.asarray(t).T.reshape(COLS, PASSES, -1, NZ).transpose(1, 0, 2, 3).reshape(PASSES, -1, NZ)
+        for t in (levels, slopes)
+    )
     return lift, slope, np.ascontiguousarray(drop), fourier_eval(KY, YG), np.ascontiguousarray(fourier_proj(KY, YG))
 
 
@@ -89,10 +93,10 @@
 
 
 def kernel(
-    vel, buoy, lift, slope, drop, evals, projs, strat, eig_val, eig_left, eig_right,
+    vel, buoy, lift, slope, drop_in, evals_in, projs_in, strat, eig_val, left_in, right_in,
     out_buoy, out_vel,
     lifted, arrived, spread, grid, returned, folded, tall, wide_eval, wide_proj, eval_x, proj_x, flux, partial,
-    strat_in,
+    strat_in, drop, evals, projs, eig_left, eig_right, load_s,
     colf_s, colf_r, rowf_s, rowf_r, rowb_s, rowb_r, colb_s, colb_r, strat_s, strat_r,
 ):
     row, col = lax.axis_index("row"), lax.axis_index("col")
@@ -116,16 +120,20 @@
     def _(i):
         pl.semaphore_signal(barrier, inc=1, device_id=row_of((row + i) % ROWS), device_id_type=MESH)
 
-    pl.semaphore_wait(barrier, COLS + ROWS - 2)
+    loads = [
+        pltpu.make_async_copy(src, dst, load_s.at[n])
+        for n, (src, dst) in enumerate(
+            ((evals_in, evals), (projs_in, projs), (drop_in, drop), (left_in, eig_left), (right_in, eig_right))
+        )
+    ]
+    for load in loads:
+        load.start()
 
     def remote(src, dst, send, recv, device):
         return pltpu.make_async_remote_copy(
             src_ref=src, dst_ref=dst, send_sem=send, recv_sem=recv, device_id=device, device_id_type=MESH
         )
 
-    swap = remote(strat, strat_in, strat_s, strat_r, (row, base + 1 - low))
-    swap.start()
-
     def col_fwd(g, q):
         return remote(lifted.at[g, q], arrived.at[g, col], colf_s.at[g, q], colf_r.at[g, col], col_of(q))
 
@@ -175,28 +183,43 @@
         def _(i):
             do((first + i) % count)
 
-    @pl.loop(0, 2)
-    def _(side):
-        count = ZG // 2
-        points = pl.ds(pl.multiple_of(side * count, count), count)
+    count = ZG // PASSES
+    chunks = G // PASSES
+
+    def to_points(u):
         for f, (table, field) in enumerate(((lift, vel), (slope, buoy))):
 
             @pl.loop(0, PAIRS // 2)
             def _(p):
                 rows = pl.ds(pl.multiple_of(p * TWO, TWO), TWO)
-                values = mm(table[points, :], field[rows, :], ((1,), (1,)))
+                values = mm(table[u], field[rows, :], ((1,), (1,)))
                 tall[pl.ds(2 * p, count, stride=PAIRS), :] = values[:, :LANES]
                 tall[pl.ds(2 * p + 1, count, stride=PAIRS), :] = values[:, LANES:]
 
-            @pl.loop(0, COLS // 2 * G)
+            @pl.loop(0, COLS * chunks)
             def _(i):
                 rows = pl.ds(pl.multiple_of(i * SIZE, SIZE), SIZE)
-                lifted[i % G, side * (COLS // 2) + i // G, f] = tall[rows, :].astype(BF)
-
-    @pl.loop(0, G)
-    def _(g):
-        others(part, COLS, lambda q: col_fwd(g, q).start())
-        col_fwd_own(g).start()
+                lifted[u * chunks + i % chunks, i // chunks, f] = tall[rows, :].astype(BF)
+
+    def send_points(u):
+        @pl.loop(u * chunks, (u + 1) * chunks)
+        def _(g):
+            others(part, COLS, lambda q: col_fwd(g, q).start())
+            col_fwd_own(g).start()
+
+    to_points(0)
+    pl.semaphore_wait(barrier, COLS + ROWS - 2)
+    send_points(0)
+    swap = remote(strat, strat_in, strat_s, strat_r, (row, base + 1 - low))
+    swap.start()
+
+    @pl.loop(1, PASSES)
+    def _(u):
+        to_points(u)
+        send_points(u)
+
+    for load in loads:
+        load.wait()
 
     @pl.loop(0, COLS)
     def _(s):
@@ -377,12 +400,13 @@
     modes = A * K
     dma = pltpu.SemaphoreType.DMA
     vmem = pl.BlockSpec(memory_space=pltpu.VMEM)
+    hbm = pl.BlockSpec(memory_space=pl.ANY)
     shape = jax.ShapeDtypeStruct((modes, NZ), BF)
     consts = [jnp.asarray(t) for t in tables()]
     new_buoy, new_vel = pl.pallas_call(
         kernel,
         out_shape=(shape, shape),
-        in_specs=[vmem] * 11,
+        in_specs=[vmem] * 4 + [hbm] * 3 + [vmem] * 2 + [hbm] * 2,
         out_specs=(vmem, vmem),
         scratch_shapes=[
             pltpu.VMEM((G, COLS, 2, SIZE, LANES), BF),
@@ -399,6 +423,12 @@
             pltpu.VMEM((XG, 2 * YH), BF),
             pltpu.VMEM((2, modes, NZ), F32),
             pltpu.VMEM((ZPART,), F32),
+            pltpu.VMEM((ZG, NZ), BF),
+            pltpu.VMEM((KY, YG), BF),
+            pltpu.VMEM((YG, KY), BF),
+            pltpu.VMEM((NZ, NZ), BF),
+            pltpu.VMEM((NZ, NZ), BF),
+            dma((5,)),
             dma((G, COLS)), dma((G, COLS)), dma((G, ROWS)), dma((G, ROWS)),
             dma((G, ROWS)), dma((G, ROWS)), dma((G, COLS)), dma((G, COLS)),
             dma, dma,

time: 224 us -> 219 us (0.978)
  Pallas kernels: 218 us -> 212 us
    pallas_call x1, Pallas kernels: 218 us -> 212 us  [per_device(): pl.pallas_call(kernel, out_shape=(shape, shape), in_specs=[vmem] * 4 + [h...]
where the time goes in v3:
time: 219 us; the launch traced here: 216 us
  Pallas kernels  212 us (97%)
  local copies, waits for them, and re-layouts  3.98 us (2%)
    pallas_call x1, Pallas kernels, per_device(): pl.pallas_call(kernel, out_shape=(shape, shape), in_specs=[vmem] * 4 + [h...  212 us

profile of v3, /device:TPU:5, one launch (start us, length us, event | category | flops | bytes accessed | tf_op | source)
XLA Modules:
  0.0 216.3 jit_solution(5902157660778693913)
XLA Ops:
  0.6 211.6 %section.1 = (bf16[2048,384]{1,0:T(8,128)(2,1)}, bf16[2048,384]{1,0:T(8,128)(2,1)}) custom-call(bf16[2048,384]{1,0:T(8,128)(2,1)} %bitcast.6, bf16[2048,384]{1,0:T(8,128)(2,1)} %bitcast.7, bf16[3,192,384]{2,1,0:T(8,128)(2,1)} %constant.10.clone.lift, bf16[3,192,384]{2,1,0:T(8,128)(2,1)} %constant.11.clone.slope, bf16[576,384]{1,0:T(8,128)(2,1)} %constant.12.clone.drop_in, ...), custom_call_target="tpu_custom_call" | custom-call | tf_op jit(solution)/shard_map/section/pallas_call | solution.py:406
  212.3 0.0 copy-start
  212.3 2.8 %copy.15 = bf16[32,64,384]{2,1,0:T(8,128)(2,1)} copy(bf16[32,64,384]{2,1,0:T(8,128)(2,1)} %bitcast.5) | data formatting | bytes 3145728
  215.1 0.0 copy-done
  215.1 1.1 copy.16
Async XLA Ops:
  212.3 2.8 %copy-start = (bf16[2048,384]{1,0:T(8,128)(2,1)S(1)}, bf16[2048,384]{1,0:T(8,128)(2,1)}, u32[]{:S(2)}) copy-start(bf16[2048,384]{1,0:T(8,128)(2,1)} %get-tuple-element.5) | copy-start | bytes 4718596

commit v4 on v3

--- a/solution.py
+++ b/solution.py
@@ -33,7 +33,6 @@
 ZPART = ZG // COLS
 ZC = ZPART // G
 SIZE = ZC * PAIRS
-YH = YG // 2
 TWO = 2 * LANES
 TALL = 5 * COLS * SIZE
 ENDS = (5, 8, 9)
@@ -80,12 +79,12 @@
 
 def tables():
     levels, slopes, projector = cheb_tables(NZ, ZG)
-    drop = np.asarray(projector).reshape(COLS, G, ZC, NZ).transpose(1, 0, 2, 3).reshape(ZG, NZ)
-    lift, slope = (
-        np.asarray(t).T.reshape(COLS, PASSES, -1, NZ).transpose(1, 0, 2, 3).reshape(PASSES, -1, NZ)
-        for t in (levels, slopes)
-    )
-    return lift, slope, np.ascontiguousarray(drop), fourier_eval(KY, YG), np.ascontiguousarray(fourier_proj(KY, YG))
+
+    def by_chunk(rows):
+        return np.asarray(rows).reshape(COLS, ZC, G, NZ).transpose(2, 0, 1, 3).reshape(ZG, NZ)
+
+    lift, slope = (by_chunk(np.asarray(t).T).reshape(PASSES, -1, NZ) for t in (levels, slopes))
+    return lift, slope, by_chunk(projector), fourier_eval(KY, YG), np.ascontiguousarray(fourier_proj(KY, YG))
 
 
 def mm(left, right, dims=((1,), (0,))):
@@ -95,7 +94,7 @@
 def kernel(
     vel, buoy, lift, slope, drop_in, evals_in, projs_in, strat, eig_val, left_in, right_in,
     out_buoy, out_vel,
-    lifted, arrived, spread, grid, returned, folded, tall, wide_eval, wide_proj, eval_x, proj_x, flux, partial,
+    lifted, arrived, planes, passed, folded, tall, wide_eval, wide_proj, eval_x, proj_x, middle, flux, partial,
     strat_in, drop, evals, projs, eig_left, eig_right, load_s,
     colf_s, colf_r, rowf_s, rowf_r, rowb_s, rowb_r, colb_s, colb_r, strat_s, strat_r,
 ):
@@ -134,54 +133,83 @@
             src_ref=src, dst_ref=dst, send_sem=send, recv_sem=recv, device_id=device, device_id_type=MESH
         )
 
+    chip, core = row // 2, row % 2
+
     def col_fwd(g, q):
-        return remote(lifted.at[g, q], arrived.at[g, col], colf_s.at[g, q], colf_r.at[g, col], col_of(q))
+        return remote(lifted.at[g, q], arrived.at[g, :, col], colf_s.at[g, q], colf_r.at[g, col], col_of(q))
 
     def col_fwd_in(g, s):
-        block = arrived.at[g, s]
+        block = arrived.at[g, :, s]
         return remote(block, block, colf_s.at[g, s], colf_r.at[g, s], col_of(0))
 
     def col_fwd_own(g):
-        return pltpu.make_async_copy(lifted.at[g, part], arrived.at[g, col], colf_r.at[g, col])
-
-    def row_fwd(g, t):
-        mine = pl.ds(pl.multiple_of(row * A, A), A)
-        return remote(spread.at[g, t], grid.at[g, :, mine, :], rowf_s.at[g, t], rowf_r.at[g, row], row_of(t))
-
-    def row_fwd_in(g, t):
-        block = grid.at[g, :, pl.ds(pl.multiple_of(t * A, A), A), :]
-        return remote(block, block, rowf_s.at[g, t], rowf_r.at[g, t], row_of(t))
-
-    def row_fwd_own(g):
-        mine = pl.ds(pl.multiple_of(row * A, A), A)
-        return pltpu.make_async_copy(spread.at[g, row], grid.at[g, :, mine, :], rowf_r.at[g, row])
-
-    def row_back(g, t):
-        theirs = pl.ds(pl.multiple_of(t * A, A), A)
-        return remote(grid.at[g, :, theirs, :], returned.at[g, row], rowb_s.at[g, t], rowb_r.at[g, row], row_of(t))
-
-    def row_back_in(g, t):
-        block = returned.at[g, t]
-        return remote(block, block, rowb_s.at[g, t], rowb_r.at[g, t], row_of(t))
-
-    def row_back_own(g):
-        mine = pl.ds(pl.multiple_of(row * A, A), A)
-        return pltpu.make_async_copy(grid.at[g, :, mine, :], returned.at[g, row], rowb_r.at[g, row])
+        return pltpu.make_async_copy(lifted.at[g, part], arrived.at[g, :, col], colf_r.at[g, col])
 
     def col_back(g, s):
-        return remote(arrived.at[g, s], folded.at[g, part], colb_s.at[g, s], colb_r.at[g, part], (row, s))
+        return remote(passed.at[g, :, s], folded.at[g, part], colb_s.at[g, s], colb_r.at[g, part], (row, s))
 
     def col_back_in(g, q):
         block = folded.at[g, q]
         return remote(block, block, colb_s.at[g, q], colb_r.at[g, q], col_of(q))
 
     def col_back_own(g):
-        return pltpu.make_async_copy(arrived.at[g, col], folded.at[g, part], colb_r.at[g, part])
+        return pltpu.make_async_copy(passed.at[g, :, col], folded.at[g, part], colb_r.at[g, part])
 
     def others(first, count, do):
         @pl.loop(1, count)
         def _(i):
             do((first + i) % count)
+
+    def row_fwd(g, t):
+        m = g // 2
+        return remote(arrived.at[g, t // 2], planes.at[m, row], rowf_s.at[m, t], rowf_r.at[m, row], row_of(t))
+
+    def row_fwd_in(m, t):
+        block = planes.at[m, t]
+        return remote(block, block, rowf_s.at[m, t], rowf_r.at[m, t], row_of(t))
+
+    def row_fwd_own(g):
+        m = g // 2
+        return pltpu.make_async_copy(arrived.at[g, chip], planes.at[m, row], rowf_r.at[m, row])
+
+    def row_back(m, g, t):
+        return remote(planes.at[m, t], passed.at[g, chip], rowb_s.at[m, t], rowb_r.at[g, chip], row_of(t))
+
+    def row_back_in(g, t):
+        block = passed.at[g, t // 2]
+        return remote(block, block, rowb_s.at[0, t], rowb_r.at[g, t // 2], row_of(t))
+
+    def row_back_own(m, g):
+        return pltpu.make_async_copy(planes.at[m, row], passed.at[g, chip], rowb_r.at[g, chip])
+
+    def chips(side, here, there):
+        @pl.loop(0, ZC)
+        def _(i):
+            t = ((chip + i) % ZC) * 2 + side
+            pl.when(t == row)(lambda: here())
+            pl.when(t != row)(lambda: there(t))
+
+    def members(here, there):
+        chips(core, here, there)
+        chips(1 - core, here, there)
+
+    def relay_fwd(g):
+        others(col, COLS, lambda s: col_fwd_in(g, s).wait_recv())
+        col_fwd_own(g).wait()
+
+        @pl.when(g < G - 1)
+        def _():
+            chips(g % 2, lambda: row_fwd_own(g).start(), lambda t: row_fwd(g, t).start())
+
+        @pl.when(g == G - 1)
+        def _():
+            members(lambda: row_fwd_own(g).start(), lambda t: row_fwd(g, t).start())
+
+    def relay_back(g):
+        side = jnp.where(g == G - 1, core, g % 2)
+        chips(side, lambda: row_back_own(0, g).wait(), lambda t: row_back_in(g, t).wait_recv())
+        others(col, COLS, lambda s: col_back(g, s).start())
+        col_back_own(g).start()
 
     count = ZG // PASSES
     chunks = G // PASSES
@@ -199,7 +227,8 @@
             @pl.loop(0, COLS * chunks)
             def _(i):
                 rows = pl.ds(pl.multiple_of(i * SIZE, SIZE), SIZE)
-                lifted[u * chunks + i % chunks, i // chunks, f] = tall[rows, :].astype(BF)
+                block = tall[rows, :].astype(BF).reshape(ZC, PAIRS, LANES)
+                lifted[u * chunks + i // COLS, i % COLS, :, f] = block
 
     def send_points(u):
         @pl.loop(u * chunks, (u + 1) * chunks)
@@ -229,22 +258,7 @@
             wide_eval[a, own, :] = evals[pl.ds(pl.multiple_of(s * K, K), K), :]
             wide_eval[a, other, :] = jnp.zeros((K, YG), BF)
 
-    @pl.loop(0, G)
-    def _(g):
-        others(col, COLS, lambda s: col_fwd_in(g, s).wait_recv())
-        col_fwd_own(g).wait()
-        left = jnp.concatenate(
-            [jnp.concatenate([arrived[g, s, f] for s in range(COLS)], axis=1) for f in range(2)], axis=0
-        )
-        for a in range(2):
-            values = mm(left, wide_eval[a]).astype(BF)
-            for f in range(2):
-                for h in range(2):
-                    block = values[f * SIZE : (f + 1) * SIZE, h * YH : (h + 1) * YH]
-                    spread[g, h * 8 : (h + 1) * 8, f, a * PAIRS : (a + 1) * PAIRS, :] = block.reshape(8, PAIRS, YH)
-
-        others(row, ROWS, lambda t: row_fwd(g, t).start())
-        row_fwd_own(g).start()
+    relay_fwd(0)
 
     lane = lax.broadcasted_iota(jnp.int32, (YG, LANES), 1)
     for j in range(COLS // 2):
@@ -262,71 +276,70 @@
 
         def ordered(values):
             tall[:KX, :] = values
-            return jnp.concatenate(
-                [tall[pl.ds(r * A + a, PAIRS, stride=2), :] for r in range(ROWS) for a in range(2)], axis=0
-            )
+            return jnp.concatenate([tall[pl.ds(a, KX // 2, stride=2), :] for a in range(2)], axis=0)
 
         eval_x[points, :] = ordered(evals[:, points].astype(F32)).T.astype(BF)
         proj_x[:, points] = ordered(projs[points, :].astype(F32).T).astype(BF)
 
+    pl.loop(1, 3)(relay_fwd)
     swap.wait()
     strata = jnp.where(high == 0, strat[...], strat_in[...]).reshape(1, ZPART)
     level_of = lax.broadcasted_iota(jnp.int32, (1, ZPART), 1)
 
-    @pl.loop(0, G)
-    def _(g):
-        others(row, ROWS, lambda t: row_fwd_in(g, t).wait_recv())
-        row_fwd_own(g).wait()
-        level = jnp.sum(jnp.where(level_of == g * ZC + row % 8, strata, 0.0), axis=1, keepdims=True)
-        right = jnp.concatenate([grid[g, 0], grid[g, 1]], axis=1)
+    half = KX // 2
+    last = G // 2
+
+    @pl.loop(0, last + 1)
+    def _(m):
+        chunk = jnp.where(m == last, G - 1, 2 * m + core)
+        members(lambda: row_fwd_own(2 * m).wait(), lambda t: row_fwd_in(m, t).wait_recv())
+        for f in range(2):
+            left = jnp.concatenate([planes[m, :, s, f].reshape(half, LANES) for s in range(COLS)], axis=1)
+            for a in range(2):
+                middle[a * half : (a + 1) * half, f * YG : (f + 1) * YG] = mm(left, wide_eval[a]).astype(BF)
+
+        pl.when(2 * m + 3 < G)(lambda: relay_fwd(2 * m + 3))
+        pl.when(m >= 2)(lambda: relay_back(2 * m - 4))
+
+        level = jnp.sum(jnp.where(level_of == chip * G + chunk, strata, 0.0), axis=1, keepdims=True)
         tile = XG // 3
         for x in range(3):
             rows = slice(x * tile, (x + 1) * tile)
-            both = mm(eval_x[rows, :], right).astype(BF).astype(F32)
-            velocity, gradient = both[:, :YH], both[:, YH:]
-            flux[rows, :YH] = (-(velocity * gradient) - level * velocity).astype(BF)
-            flux[rows, YH:] = (-(velocity * jnp.abs(velocity))).astype(BF)
-        for x in range(2):
-            rows = slice(x * KX // 2, (x + 1) * KX // 2)
-            both = mm(proj_x[rows, :], flux[...]).astype(BF)
-            grid[g, 0, rows, :] = both[:, :YH]
-            grid[g, 1, rows, :] = both[:, YH:]
-
-        others(row, ROWS, lambda t: row_back(g, t).start())
-        row_back_own(g).start()
-
-    def to_modes(g):
-        others(row, ROWS, lambda t: row_back_in(g, t).wait_recv())
-        row_back_own(g).wait()
-
-        def side(f, a, h):
-            return returned[g, h * 8 : (h + 1) * 8, f, a * PAIRS : (a + 1) * PAIRS, :].reshape(SIZE, YH)
-
-        left = jnp.concatenate(
-            [
-                jnp.concatenate([side(f, a, h) for a in range(2) for h in range(2)], axis=1)
-                for f in range(2)
-            ],
-            axis=0,
-        )
-        half = COLS * LANES // 2
-        for n in range(2):
-            values = mm(left, wide_proj[:, n * half : (n + 1) * half]).astype(BF)
+            velocity = mm(eval_x[rows, :], middle[:, :YG]).astype(BF).astype(F32)
+            gradient = mm(eval_x[rows, :], middle[:, YG:]).astype(BF).astype(F32)
+            flux[rows, :YG] = (-(velocity * gradient) - level * velocity).astype(BF)
+            flux[rows, YG:] = (-(velocity * jnp.abs(velocity))).astype(BF)
+
+        pl.when(2 * m + 4 < G)(lambda: relay_fwd(2 * m + 4))
+        pl.when(m >= 2)(lambda: relay_back(2 * m - 3))
+
+        for a in range(2):
+            rows = slice(a * half, (a + 1) * half)
             for f in range(2):
-                for s in range(COLS // 2):
-                    arrived[g, n * COLS // 2 + s, f] = values[
-                        f * SIZE : (f + 1) * SIZE, s * LANES : (s + 1) * LANES
-                    ]
-
-        others(col, COLS, lambda s: col_back(g, s).start())
-        col_back_own(g).start()
+                middle[rows, f * YG : (f + 1) * YG] = mm(proj_x[rows, :], flux[:, f * YG : (f + 1) * YG]).astype(BF)
+        for f in range(2):
+            left = jnp.concatenate(
+                [middle[a * half : (a + 1) * half, f * YG : (f + 1) * YG] for a in range(2)], axis=1
+            )
+            values = mm(left, wide_proj[...]).astype(BF)
+            for s in range(COLS):
+                planes[m, :, s, f] = values[:, s * LANES : (s + 1) * LANES].reshape(ROWS, PAIRS, LANES)
+
+        def here():
+            row_back_own(m, chunk).start()
+
+        def there(t):
+            row_back(m, chunk, t).start()
+
+        chips(core, here, there)
+        pl.when(m < last)(lambda: chips(1 - core, here, there))
 
     def gather(first, last, f, start):
         @pl.loop(first, last)
         def _(g):
             for q in range(COLS):
                 place = pl.multiple_of(start + ((g - first) * COLS + q) * SIZE, SIZE)
-                tall[pl.ds(place, SIZE), :] = folded[g, q, f].astype(F32)
+                tall[pl.ds(place, SIZE), :] = folded[g, q, :, f].reshape(SIZE, LANES).astype(F32)
 
     def tendency(first, last, p, start):
         count = (last - first) * COLS * ZC
@@ -340,7 +353,7 @@
             others(part, COLS, lambda q: col_back_in(g, q).wait_recv())
             col_back_own(g).wait()
 
-    pl.loop(0, ENDS[0] + 1)(to_modes)
+    pl.loop(2 * last - 2, G)(relay_back)
     wait_modes(0, ENDS[0])
     for f in range(2):
         gather(0, ENDS[0], f, 0)
@@ -350,7 +363,6 @@
             rows = pl.ds(pl.multiple_of(p * TWO, TWO), TWO)
             partial[f, rows, :] = tendency(0, ENDS[0], p, 0)
 
-    pl.loop(ENDS[0] + 1, ENDS[1] + 1)(to_modes)
     wait_modes(ENDS[0], ENDS[1])
     for f in range(2):
         gather(ENDS[0], ENDS[1], f, 0)
@@ -360,7 +372,6 @@
             rows = pl.ds(pl.multiple_of(p * TWO, TWO), TWO)
             partial[f, rows, :] += tendency(ENDS[0], ENDS[1], p, 0)
 
-    pl.loop(ENDS[1] + 1, G)(to_modes)
     wait_modes(ENDS[1], G)
     start = (G - ENDS[1]) * COLS * SIZE
     for f in range(2):
@@ -391,9 +402,18 @@
     @pl.loop(0, G)
     def _(g):
         others(part, COLS, lambda q: col_fwd(g, q).wait_send())
-        others(row, ROWS, lambda t: row_fwd(g, t).wait_send())
-        others(row, ROWS, lambda t: row_back(g, t).wait_send())
         others(col, COLS, lambda s: col_back(g, s).wait_send())
+
+    def nothing():
+        pass
+
+    @pl.loop(0, last)
+    def _(m):
+        members(nothing, lambda t: row_fwd(2 * m, t).wait_send())
+        members(nothing, lambda t: row_back(m, 2 * m, t).wait_send())
+
+    members(nothing, lambda t: row_fwd(G - 1, t).wait_send())
+    chips(core, nothing, lambda t: row_back(last, G - 1, t).wait_send())
 
 
 def per_device(buoy, vel_w, strat, eig_val, eig_left, eig_right):
@@ -409,18 +429,18 @@
         in_specs=[vmem] * 4 + [hbm] * 3 + [vmem] * 2 + [hbm] * 2,
         out_specs=(vmem, vmem),
         scratch_shapes=[
-            pltpu.VMEM((G, COLS, 2, SIZE, LANES), BF),
-            pltpu.VMEM((G, COLS, 2, SIZE, LANES), BF),
-            pltpu.VMEM((G, ROWS, 2, A, YH), BF),
-            pltpu.VMEM((G, 2, KX, YH), BF),
-            pltpu.VMEM((G, ROWS, 2, A, YH), BF),
-            pltpu.VMEM((G, COLS, 2, SIZE, LANES), BF),
+            pltpu.VMEM((G, COLS, ZC, 2, PAIRS, LANES), BF),
+            pltpu.VMEM((G, ZC, COLS, 2, PAIRS, LANES), BF),
+            pltpu.VMEM((G // 2 + 1, ROWS, COLS, 2, PAIRS, LANES), BF),
+            pltpu.VMEM((G, ZC, COLS, 2, PAIRS, LANES), BF),
+            pltpu.VMEM((G, COLS, ZC, 2, PAIRS, LANES), BF),
             pltpu.VMEM((TALL, LANES), F32),
             pltpu.VMEM((2, COLS * LANES, YG), BF),
             pltpu.VMEM((2 * YG, COLS * LANES), BF),
             pltpu.VMEM((XG, KX), BF),
             pltpu.VMEM((KX, XG), BF),
-            pltpu.VMEM((XG, 2 * YH), BF),
+            pltpu.VMEM((KX, 2 * YG), BF),
+            pltpu.VMEM((XG, 2 * YG), BF),
             pltpu.VMEM((2, modes, NZ), F32),
             pltpu.VMEM((ZPART,), F32),
             pltpu.VMEM((ZG, NZ), BF),
@@ -429,8 +449,8 @@
             pltpu.VMEM((NZ, NZ), BF),
             pltpu.VMEM((NZ, NZ), BF),
             dma((5,)),
-            dma((G, COLS)), dma((G, COLS)), dma((G, ROWS)), dma((G, ROWS)),
-            dma((G, ROWS)), dma((G, ROWS)), dma((G, COLS)), dma((G, COLS)),
+            dma((G, COLS)), dma((G, COLS)), dma((G // 2 + 1, ROWS)), dma((G // 2 + 1, ROWS)),
+            dma((G // 2 + 1, ROWS)), dma((G, ZC)), dma((G, COLS)), dma((G, COLS)),
             dma, dma,
         ],
         compiler_params=pltpu.CompilerParams(

time: 219 us -> 186 us (0.85)
  Pallas kernels: 212 us -> 178 us
    pallas_call x1, Pallas kernels: 212 us -> 178 us  [per_device(): pl.pallas_call(kernel, out_shape=(shape, shape), in_specs=[vmem] * 4 + [h...]
where the time goes in v4:
time: 186 us; the launch traced here: 183 us
  Pallas kernels  178 us (96%)
  local copies, waits for them, and re-layouts  3.98 us (2%)
    pallas_call x1, Pallas kernels, per_device(): pl.pallas_call(kernel, out_shape=(shape, shape), in_specs=[vmem] * 4 + [h...  178 us
    unnamed x4, local copies, waits for them, and re-layouts  3.98 us

profile of v4, /device:TPU:5, one launch (start us, length us, event | category | flops | bytes accessed | tf_op | source)
XLA Modules:
  0.0 182.5 jit_solution(17672121130653788830)
XLA Ops:
  0.6 177.9 %section.1 = (bf16[2048,384]{1,0:T(8,128)(2,1)}, bf16[2048,384]{1,0:T(8,128)(2,1)}) custom-call(bf16[2048,384]{1,0:T(8,128)(2,1)} %bitcast.6, bf16[2048,384]{1,0:T(8,128)(2,1)} %bitcast.7, bf16[3,192,384]{2,1,0:T(8,128)(2,1)} %constant.10.clone.lift, bf16[3,192,384]{2,1,0:T(8,128)(2,1)} %constant.11.clone.slope, bf16[576,384]{1,0:T(8,128)(2,1)} %constant.12.clone.drop_in, ...), custom_call_target="tpu_custom_call" | custom-call | tf_op jit(solution)/shard_map/section/pallas_call | solution.py:426
  178.5 0.0 copy-start
  178.6 2.8 %copy.15 = bf16[32,64,384]{2,1,0:T(8,128)(2,1)} copy(bf16[32,64,384]{2,1,0:T(8,128)(2,1)} %bitcast.5) | data formatting | bytes 3145728
  181.4 0.0 copy-done
  181.4 1.1 copy.16
Async XLA Ops:
  178.5 2.8 %copy-start = (bf16[2048,384]{1,0:T(8,128)(2,1)S(1)}, bf16[2048,384]{1,0:T(8,128)(2,1)}, u32[]{:S(2)}) copy-start(bf16[2048,384]{1,0:T(8,128)(2,1)} %get-tuple-element.5) | copy-start | bytes 4718596

commit v5 on v4

--- a/solution.py
+++ b/solution.py
@@ -34,8 +34,8 @@
 ZC = ZPART // G
 SIZE = ZC * PAIRS
 TWO = 2 * LANES
-TALL = 5 * COLS * SIZE
-ENDS = (5, 8, 9)
+TALL = 4 * COLS * SIZE
+ENDS = (4, 8, 9)
 BF = jnp.bfloat16
 F32 = jnp.float32
 MESH = pl.DeviceIdType.MESH
@@ -260,15 +260,20 @@
 
     relay_fwd(0)
 
-    lane = lax.broadcasted_iota(jnp.int32, (YG, LANES), 1)
-    for j in range(COLS // 2):
-        tile = projs[:, j * LANES : (j + 1) * LANES].astype(F32)
-        turned = pltpu.roll(tile, K, 1)
-        for s in (2 * j, 2 * j + 1):
-            straight, moved = (tile, turned) if s % 2 == 0 else (turned, tile)
-            for a in range(2):
-                keep = jnp.where((lane < K) == (a == 0), straight if a == 0 else moved, 0.0).astype(BF)
-                wide_proj[a * YG : (a + 1) * YG, s * LANES : (s + 1) * LANES] = keep
+    lane = lax.broadcasted_iota(jnp.int32, (LANES, LANES), 1)
+
+    @pl.loop(0, YG // LANES)
+    def _(i):
+        for j in range(COLS // 2):
+            rows = pl.ds(pl.multiple_of(i * LANES, LANES), LANES)
+            tile = projs[rows, j * LANES : (j + 1) * LANES].astype(F32)
+            turned = pltpu.roll(tile, K, 1)
+            for s in (2 * j, 2 * j + 1):
+                straight, moved = (tile, turned) if s % 2 == 0 else (turned, tile)
+                for a in range(2):
+                    keep = jnp.where((lane < K) == (a == 0), straight if a == 0 else moved, 0.0).astype(BF)
+                    to = pl.ds(pl.multiple_of(a * YG + i * LANES, LANES), LANES)
+                    wide_proj[to, s * LANES : (s + 1) * LANES] = keep
 
     @pl.loop(0, XG // LANES)
     def _(j):
@@ -281,7 +286,7 @@
         eval_x[points, :] = ordered(evals[:, points].astype(F32)).T.astype(BF)
         proj_x[:, points] = ordered(projs[points, :].astype(F32).T).astype(BF)
 
-    pl.loop(1, 3)(relay_fwd)
+    pl.loop(1, 5)(relay_fwd)
     swap.wait()
     strata = jnp.where(high == 0, strat[...], strat_in[...]).reshape(1, ZPART)
     level_of = lax.broadcasted_iota(jnp.int32, (1, ZPART), 1)
@@ -298,23 +303,24 @@
             for a in range(2):
                 middle[a * half : (a + 1) * half, f * YG : (f + 1) * YG] = mm(left, wide_eval[a]).astype(BF)
 
-        pl.when(2 * m + 3 < G)(lambda: relay_fwd(2 * m + 3))
-        pl.when(m >= 2)(lambda: relay_back(2 * m - 4))
+        pl.when(2 * m + 5 < G)(lambda: relay_fwd(2 * m + 5))
 
         level = jnp.sum(jnp.where(level_of == chip * G + chunk, strata, 0.0), axis=1, keepdims=True)
         tile = XG // 3
-        for x in range(3):
-            rows = slice(x * tile, (x + 1) * tile)
+
+        @pl.loop(0, 3)
+        def _(x):
+            rows = pl.ds(pl.multiple_of(x * tile, tile), tile)
             velocity = mm(eval_x[rows, :], middle[:, :YG]).astype(BF).astype(F32)
             gradient = mm(eval_x[rows, :], middle[:, YG:]).astype(BF).astype(F32)
             flux[rows, :YG] = (-(velocity * gradient) - level * velocity).astype(BF)
             flux[rows, YG:] = (-(velocity * jnp.abs(velocity))).astype(BF)
 
-        pl.when(2 * m + 4 < G)(lambda: relay_fwd(2 * m + 4))
-        pl.when(m >= 2)(lambda: relay_back(2 * m - 3))
-
-        for a in range(2):
-            rows = slice(a * half, (a + 1) * half)
+        pl.when(2 * m + 6 < G)(lambda: relay_fwd(2 * m + 6))
+
+        @pl.loop(0, 2)
+        def _(a):
+            rows = pl.ds(pl.multiple_of(a * half, half), half)
             for f in range(2):
                 middle[rows, f * YG : (f + 1) * YG] = mm(proj_x[rows, :], flux[:, f * YG : (f + 1) * YG]).astype(BF)
         for f in range(2):
@@ -334,6 +340,10 @@
         chips(core, here, there)
         pl.when(m < last)(lambda: chips(1 - core, here, there))
 
+        @pl.when(m == last - 1)
+        def _():
+            pl.loop(0, 2)(relay_back)
+
     def gather(first, last, f, start):
         @pl.loop(first, last)
         def _(g):
@@ -353,7 +363,7 @@
             others(part, COLS, lambda q: col_back_in(g, q).wait_recv())
             col_back_own(g).wait()
 
-    pl.loop(2 * last - 2, G)(relay_back)
+    pl.loop(2, ENDS[0] + 2)(relay_back)
     wait_modes(0, ENDS[0])
     for f in range(2):
         gather(0, ENDS[0], f, 0)
@@ -363,6 +373,7 @@
             rows = pl.ds(pl.multiple_of(p * TWO, TWO), TWO)
             partial[f, rows, :] = tendency(0, ENDS[0], p, 0)
 
+    pl.loop(ENDS[0] + 2, G)(relay_back)
     wait_modes(ENDS[0], ENDS[1])
     for f in range(2):
         gather(ENDS[0], ENDS[1], f, 0)

time: 186 us -> 175 us (0.941); the launches traced: 183 us -> 175 us
  Pallas kernels: 178 us -> 170 us
    pallas_call x1, Pallas kernels: 178 us -> 170 us  [per_device(): pl.pallas_call(kernel, out_shape=(shape, shape), in_specs=[vmem] * 4 + [h...]
where the time goes in v5:
time: 175 us
  Pallas kernels  170 us (97%)
  local copies, waits for them, and re-layouts  3.98 us (2%)
    pallas_call x1, Pallas kernels, per_device(): pl.pallas_call(kernel, out_shape=(shape, shape), in_specs=[vmem] * 4 + [h...  170 us
    unnamed x4, local copies, waits for them, and re-layouts  3.98 us

profile of v5, /device:TPU:5, one launch (start us, length us, event | category | flops | bytes accessed | tf_op | source)
XLA Modules:
  0.0 174.7 jit_solution(13989448534589565134)
XLA Ops:
  0.6 170.1 %section.1 = (bf16[2048,384]{1,0:T(8,128)(2,1)}, bf16[2048,384]{1,0:T(8,128)(2,1)}) custom-call(bf16[2048,384]{1,0:T(8,128)(2,1)} %bitcast.6, bf16[2048,384]{1,0:T(8,128)(2,1)} %bitcast.7, bf16[3,192,384]{2,1,0:T(8,128)(2,1)} %constant.10.clone.lift, bf16[3,192,384]{2,1,0:T(8,128)(2,1)} %constant.11.clone.slope, bf16[576,384]{1,0:T(8,128)(2,1)} %constant.12.clone.drop_in, ...), custom_call_target="tpu_custom_call" | custom-call | tf_op jit(solution)/shard_map/section/pallas_call | solution.py:437
  170.7 0.0 copy-start
  170.7 2.8 %copy.15 = bf16[32,64,384]{2,1,0:T(8,128)(2,1)} copy(bf16[32,64,384]{2,1,0:T(8,128)(2,1)} %bitcast.5) | data formatting | bytes 3145728
  173.5 0.0 copy-done
  173.5 1.1 copy.16
Async XLA Ops:
  170.7 2.8 %copy-start = (bf16[2048,384]{1,0:T(8,128)(2,1)S(1)}, bf16[2048,384]{1,0:T(8,128)(2,1)}, u32[]{:S(2)}) copy-start(bf16[2048,384]{1,0:T(8,128)(2,1)} %get-tuple-element.5) | copy-start | bytes 4718596

commit v6 on v5

--- a/solution.py
+++ b/solution.py
@@ -197,17 +197,10 @@
         others(col, COLS, lambda s: col_fwd_in(g, s).wait_recv())
         col_fwd_own(g).wait()
 
-        @pl.when(g < G - 1)
-        def _():
-            chips(g % 2, lambda: row_fwd_own(g).start(), lambda t: row_fwd(g, t).start())
-
-        @pl.when(g == G - 1)
-        def _():
-            members(lambda: row_fwd_own(g).start(), lambda t: row_fwd(g, t).start())
+        chips(g % 2, lambda: row_fwd_own(g).start(), lambda t: row_fwd(g, t).start())
 
     def relay_back(g):
-        side = jnp.where(g == G - 1, core, g % 2)
-        chips(side, lambda: row_back_own(0, g).wait(), lambda t: row_back_in(g, t).wait_recv())
+        chips(g % 2, lambda: row_back_own(0, g).wait(), lambda t: row_back_in(g, t).wait_recv())
         others(col, COLS, lambda s: col_back(g, s).start())
         col_back_own(g).start()
 
@@ -294,9 +287,9 @@
     half = KX // 2
     last = G // 2
 
-    @pl.loop(0, last + 1)
+    @pl.loop(0, last + 1 - core)
     def _(m):
-        chunk = jnp.where(m == last, G - 1, 2 * m + core)
+        chunk = 2 * m + core
         members(lambda: row_fwd_own(2 * m).wait(), lambda t: row_fwd_in(m, t).wait_recv())
         for f in range(2):
             left = jnp.concatenate([planes[m, :, s, f].reshape(half, LANES) for s in range(COLS)], axis=1)
@@ -331,14 +324,7 @@
             for s in range(COLS):
                 planes[m, :, s, f] = values[:, s * LANES : (s + 1) * LANES].reshape(ROWS, PAIRS, LANES)
 
-        def here():
-            row_back_own(m, chunk).start()
-
-        def there(t):
-            row_back(m, chunk, t).start()
-
-        chips(core, here, there)
-        pl.when(m < last)(lambda: chips(1 - core, here, there))
+        members(lambda: row_back_own(m, chunk).start(), lambda t: row_back(m, chunk, t).start())
 
         @pl.when(m == last - 1)
         def _():
@@ -421,10 +407,12 @@
     @pl.loop(0, last)
     def _(m):
         members(nothing, lambda t: row_fwd(2 * m, t).wait_send())
+
+    @pl.loop(0, last + 1 - core)
+    def _(m):
         members(nothing, lambda t: row_back(m, 2 * m, t).wait_send())
 
-    members(nothing, lambda t: row_fwd(G - 1, t).wait_send())
-    chips(core, nothing, lambda t: row_back(last, G - 1, t).wait_send())
+    chips(0, nothing, lambda t: row_fwd(G - 1, t).wait_send())
 
 
 def per_device(buoy, vel_w, strat, eig_val, eig_left, eig_right):

time: 175 us -> 170 us (0.971)
  Pallas kernels: 170 us -> 164 us
    pallas_call x1, Pallas kernels: 170 us -> 164 us  [per_device(): pl.pallas_call(kernel, out_shape=(shape, shape), in_specs=[vmem] * 4 + [h...]
where the time goes in v6:
time: 170 us; the launch traced here: 168 us
  Pallas kernels  164 us (96%)
  local copies, waits for them, and re-layouts  3.98 us (2%)
    pallas_call x1, Pallas kernels, per_device(): pl.pallas_call(kernel, out_shape=(shape, shape), in_specs=[vmem] * 4 + [h...  164 us
    unnamed x4, local copies, waits for them, and re-layouts  3.98 us

profile of v6, /device:TPU:5, one launch (start us, length us, event | category | flops | bytes accessed | tf_op | source)
XLA Modules:
  0.0 168.2 jit_solution(914025300761696798)
XLA Ops:
  0.6 163.6 %section.1 = (bf16[2048,384]{1,0:T(8,128)(2,1)}, bf16[2048,384]{1,0:T(8,128)(2,1)}) custom-call(bf16[2048,384]{1,0:T(8,128)(2,1)} %bitcast.6, bf16[2048,384]{1,0:T(8,128)(2,1)} %bitcast.7, bf16[3,192,384]{2,1,0:T(8,128)(2,1)} %constant.10.clone.lift, bf16[3,192,384]{2,1,0:T(8,128)(2,1)} %constant.11.clone.slope, bf16[576,384]{1,0:T(8,128)(2,1)} %constant.12.clone.drop_in, ...), custom_call_target="tpu_custom_call" | custom-call | tf_op jit(solution)/shard_map/section/pallas_call | solution.py:425
  164.2 0.0 copy-start
  164.2 2.8 %copy.15 = bf16[32,64,384]{2,1,0:T(8,128)(2,1)} copy(bf16[32,64,384]{2,1,0:T(8,128)(2,1)} %bitcast.5) | data formatting | bytes 3145728
  167.0 0.0 copy-done
  167.0 1.1 copy.16
Async XLA Ops:
  164.2 2.8 %copy-start = (bf16[2048,384]{1,0:T(8,128)(2,1)S(1)}, bf16[2048,384]{1,0:T(8,128)(2,1)}, u32[]{:S(2)}) copy-start(bf16[2048,384]{1,0:T(8,128)(2,1)} %get-tuple-element.5) | copy-start | bytes 4718596

commit v7 on v6

--- a/solution.py
+++ b/solution.py
@@ -35,6 +35,8 @@
 SIZE = ZC * PAIRS
 TWO = 2 * LANES
 TALL = 4 * COLS * SIZE
+ORDER = (0, 6, 7, 1, 2, 3, 4, 5, 8)
+TURN = 3
 ENDS = (4, 8, 9)
 BF = jnp.bfloat16
 F32 = jnp.float32
@@ -83,7 +85,9 @@
     def by_chunk(rows):
         return np.asarray(rows).reshape(COLS, ZC, G, NZ).transpose(2, 0, 1, 3).reshape(ZG, NZ)
 
-    lift, slope = (by_chunk(np.asarray(t).T).reshape(PASSES, -1, NZ) for t in (levels, slopes))
+    lift, slope = (
+        by_chunk(np.asarray(t).T).reshape(G, -1, NZ)[list(ORDER)].reshape(PASSES, -1, NZ) for t in (levels, slopes)
+    )
     return lift, slope, by_chunk(projector), fourier_eval(KY, YG), np.ascontiguousarray(fourier_proj(KY, YG))
 
 
@@ -96,7 +100,7 @@
     out_buoy, out_vel,
     lifted, arrived, planes, passed, folded, tall, wide_eval, wide_proj, eval_x, proj_x, middle, flux, partial,
     strat_in, drop, evals, projs, eig_left, eig_right, load_s,
-    colf_s, colf_r, rowf_s, rowf_r, rowb_s, rowb_r, colb_s, colb_r, strat_s, strat_r,
+    turn_s, turn_r, hop_s, hop_r, colf_s, colf_r, rowf_s, rowf_r, rowb_s, rowb_r, colb_s, colb_r, strat_s, strat_r,
 ):
     row, col = lax.axis_index("row"), lax.axis_index("col")
     high = row // (ROWS // 2)
@@ -193,6 +197,36 @@
         chips(core, here, there)
         chips(1 - core, here, there)
 
+    def turn_out(g, t):
+        return remote(
+            lifted.at[g, t // 2], arrived.at[2 * TURN + high, row % 8], turn_s.at[g % 2, t // 2], turn_r.at[row], row_of(t)
+        )
+
+    def turn_own(g):
+        return pltpu.make_async_copy(lifted.at[g, chip], arrived.at[2 * TURN + high, row % 8], turn_r.at[row])
+
+    def turn_in(t):
+        block = arrived.at[2 * TURN + t // 8, t % 8]
+        return remote(block, block, turn_s.at[0, 0], turn_r.at[t], row_of(t))
+
+    def landing(h, s):
+        return planes.at[TURN, h * 8 : (h + 1) * 8, (s // 2) * 2 + (s % 2 + high + h) % 2]
+
+    def hop(h, q):
+        return remote(arrived.at[2 * TURN + h, :, q], landing(h, col), hop_s.at[h, q], hop_r.at[h, col], col_of(q))
+
+    def hop_in(h, s):
+        return remote(landing(h, s), landing(h, s), hop_s.at[h, s], hop_r.at[h, s], col_of(0))
+
+    def hop_own(h):
+        return pltpu.make_async_copy(arrived.at[2 * TURN + h, :, part], landing(h, col), hop_r.at[h, col])
+
+    def relay_turned():
+        members(lambda: turn_own(2 * TURN).wait(), lambda t: turn_in(t).wait_recv())
+        for h in range(2):
+            others(part, COLS, lambda q: hop(h, q).start())
+            hop_own(h).start()
+
     def relay_fwd(g):
         others(col, COLS, lambda s: col_fwd_in(g, s).wait_recv())
         col_fwd_own(g).wait()
@@ -206,6 +240,9 @@
 
     count = ZG // PASSES
     chunks = G // PASSES
+
+    def chunk_at(i):
+        return jnp.where(i == 0, 0, jnp.where(i < 3, i + 5, jnp.where(i < 8, i - 2, 8)))
 
     def to_points(u):
         for f, (table, field) in enumerate(((lift, vel), (slope, buoy))):
@@ -221,13 +258,29 @@
             def _(i):
                 rows = pl.ds(pl.multiple_of(i * SIZE, SIZE), SIZE)
                 block = tall[rows, :].astype(BF).reshape(ZC, PAIRS, LANES)
-                lifted[u * chunks + i // COLS, i % COLS, :, f] = block
+                g, q = chunk_at(u * chunks + i // COLS), i % COLS
+
+                @pl.when(g // 2 != TURN)
+                def _():
+                    lifted[g, q, :, f] = block
+
+                @pl.when(g // 2 == TURN)
+                def _():
+                    lifted[g, :, q, f] = block
 
     def send_points(u):
         @pl.loop(u * chunks, (u + 1) * chunks)
-        def _(g):
-            others(part, COLS, lambda q: col_fwd(g, q).start())
-            col_fwd_own(g).start()
+        def _(i):
+            g = chunk_at(i)
+
+            @pl.when(g // 2 != TURN)
+            def _():
+                others(part, COLS, lambda q: col_fwd(g, q).start())
+                col_fwd_own(g).start()
+
+            @pl.when(g // 2 == TURN)
+            def _():
+                chips(g % 2, lambda: turn_own(g).start(), lambda t: turn_out(g, t).start())
 
     to_points(0)
     pl.semaphore_wait(barrier, COLS + ROWS - 2)
@@ -268,6 +321,8 @@
                     to = pl.ds(pl.multiple_of(a * YG + i * LANES, LANES), LANES)
                     wide_proj[to, s * LANES : (s + 1) * LANES] = keep
 
+    relay_fwd(1)
+
     @pl.loop(0, XG // LANES)
     def _(j):
         points = pl.ds(pl.multiple_of(j * LANES, LANES), LANES)
@@ -279,7 +334,8 @@
         eval_x[points, :] = ordered(evals[:, points].astype(F32)).T.astype(BF)
         proj_x[:, points] = ordered(projs[points, :].astype(F32).T).astype(BF)
 
-    pl.loop(1, 5)(relay_fwd)
+    pl.loop(2, 5)(relay_fwd)
+    relay_turned()
     swap.wait()
     strata = jnp.where(high == 0, strat[...], strat_in[...]).reshape(1, ZPART)
     level_of = lax.broadcasted_iota(jnp.int32, (1, ZPART), 1)
@@ -290,13 +346,23 @@
     @pl.loop(0, last + 1 - core)
     def _(m):
         chunk = 2 * m + core
-        members(lambda: row_fwd_own(2 * m).wait(), lambda t: row_fwd_in(m, t).wait_recv())
+
+        @pl.when(m != TURN)
+        def _():
+            members(lambda: row_fwd_own(2 * m).wait(), lambda t: row_fwd_in(m, t).wait_recv())
+
+        @pl.when(m == TURN)
+        def _():
+            for h in range(2):
+                others(col, COLS, lambda s: hop_in(h, s).wait_recv())
+                hop_own(h).wait()
+
         for f in range(2):
             left = jnp.concatenate([planes[m, :, s, f].reshape(half, LANES) for s in range(COLS)], axis=1)
             for a in range(2):
                 middle[a * half : (a + 1) * half, f * YG : (f + 1) * YG] = mm(left, wide_eval[a]).astype(BF)
 
-        pl.when(2 * m + 5 < G)(lambda: relay_fwd(2 * m + 5))
+        pl.when(m < 2)(lambda: relay_fwd(5 + 3 * m))
 
         level = jnp.sum(jnp.where(level_of == chip * G + chunk, strata, 0.0), axis=1, keepdims=True)
         tile = XG // 3
@@ -309,7 +375,6 @@
             flux[rows, :YG] = (-(velocity * gradient) - level * velocity).astype(BF)
             flux[rows, YG:] = (-(velocity * jnp.abs(velocity))).astype(BF)
 
-        pl.when(2 * m + 6 < G)(lambda: relay_fwd(2 * m + 6))
 
         @pl.loop(0, 2)
         def _(a):
@@ -396,17 +461,27 @@
         out_buoy[rows, :] = mm(solved_buoy, eig_right[...]).astype(BF)
         out_vel[rows, :] = mm(solved_vel, eig_right[...]).astype(BF)
 
+    def nothing():
+        pass
+
+    for h in range(2):
+        others(part, COLS, lambda q: hop(h, q).wait_send())
+
     @pl.loop(0, G)
     def _(g):
-        others(part, COLS, lambda q: col_fwd(g, q).wait_send())
+        @pl.when(g // 2 != TURN)
+        def _():
+            others(part, COLS, lambda q: col_fwd(g, q).wait_send())
+
+        @pl.when(g // 2 == TURN)
+        def _():
+            chips(g % 2, nothing, lambda t: turn_out(g, t).wait_send())
+
         others(col, COLS, lambda s: col_back(g, s).wait_send())
-
-    def nothing():
-        pass
 
     @pl.loop(0, last)
     def _(m):
-        members(nothing, lambda t: row_fwd(2 * m, t).wait_send())
+        pl.when(m != TURN)(lambda: members(nothing, lambda t: row_fwd(2 * m, t).wait_send()))
 
     @pl.loop(0, last + 1 - core)
     def _(m):
@@ -447,7 +522,7 @@
             pltpu.VMEM((YG, KY), BF),
             pltpu.VMEM((NZ, NZ), BF),
             pltpu.VMEM((NZ, NZ), BF),
-            dma((5,)),
+            dma((5,)), dma((2, ZC)), dma((ROWS,)), dma((2, COLS)), dma((2, COLS)),
             dma((G, COLS)), dma((G, COLS)), dma((G // 2 + 1, ROWS)), dma((G // 2 + 1, ROWS)),
             dma((G // 2 + 1, ROWS)), dma((G, ZC)), dma((G, COLS)), dma((G, COLS)),
             dma, dma,

time: 170 us -> 163 us (0.959)
  Pallas kernels: 164 us -> 156 us
    pallas_call x1, Pallas kernels: 164 us -> 156 us  [per_device(): pl.pallas_call(kernel, out_shape=(shape, shape), in_specs=[vmem] * 4 + [h...]
where the time goes in v7:
time: 163 us; the launch traced here: 161 us
  Pallas kernels  156 us (96%)
  local copies, waits for them, and re-layouts  3.98 us (2%)
    pallas_call x1, Pallas kernels, per_device(): pl.pallas_call(kernel, out_shape=(shape, shape), in_specs=[vmem] * 4 + [h...  156 us
    unnamed x4, local copies, waits for them, and re-layouts  3.98 us

profile of v7, /device:TPU:5, one launch (start us, length us, event | category | flops | bytes accessed | tf_op | source)
XLA Modules:
  0.0 160.8 jit_solution(8818311028763379722)
XLA Ops:
  0.6 156.2 %section.1 = (bf16[2048,384]{1,0:T(8,128)(2,1)}, bf16[2048,384]{1,0:T(8,128)(2,1)}) custom-call(bf16[2048,384]{1,0:T(8,128)(2,1)} %bitcast.6, bf16[2048,384]{1,0:T(8,128)(2,1)} %bitcast.7, bf16[3,192,384]{2,1,0:T(8,128)(2,1)} %constant.10.clone.lift, bf16[3,192,384]{2,1,0:T(8,128)(2,1)} %constant.11.clone.slope, bf16[576,384]{1,0:T(8,128)(2,1)} %constant.12.clone.drop_in, ...), custom_call_target="tpu_custom_call" | custom-call | tf_op jit(solution)/shard_map/section/pallas_call | solution.py:500
  156.8 0.0 copy-start
  156.8 2.8 %copy.15 = bf16[32,64,384]{2,1,0:T(8,128)(2,1)} copy(bf16[32,64,384]{2,1,0:T(8,128)(2,1)} %bitcast.5) | data formatting | bytes 3145728
  159.6 0.0 copy-done
  159.6 1.1 copy.16
Async XLA Ops:
  156.8 2.8 %copy-start = (bf16[2048,384]{1,0:T(8,128)(2,1)S(1)}, bf16[2048,384]{1,0:T(8,128)(2,1)}, u32[]{:S(2)}) copy-start(bf16[2048,384]{1,0:T(8,128)(2,1)} %get-tuple-element.5) | copy-start | bytes 4718596

commit v8 on v7

--- a/solution.py
+++ b/solution.py
@@ -99,7 +99,7 @@
     vel, buoy, lift, slope, drop_in, evals_in, projs_in, strat, eig_val, left_in, right_in,
     out_buoy, out_vel,
     lifted, arrived, planes, passed, folded, tall, wide_eval, wide_proj, eval_x, proj_x, middle, flux, partial,
-    strat_in, drop, evals, projs, eig_left, eig_right, load_s,
+    inverses, done, done_s, strat_in, drop, evals, projs, eig_left, eig_right, load_s,
     turn_s, turn_r, hop_s, hop_r, colf_s, colf_r, rowf_s, rowf_r, rowb_s, rowb_r, colb_s, colb_r, strat_s, strat_r,
 ):
     row, col = lax.axis_index("row"), lax.axis_index("col")
@@ -334,7 +334,27 @@
         eval_x[points, :] = ordered(evals[:, points].astype(F32)).T.astype(BF)
         proj_x[:, points] = ordered(projs[points, :].astype(F32).T).astype(BF)
 
-    pl.loop(2, 5)(relay_fwd)
+    relay_fwd(2)
+
+    def diagonals(p):
+        place = p * TWO + lax.broadcasted_iota(jnp.int32, (TWO, LANES), 0)
+        freq_x = ((row * A + (place >> 6) + 1) >> 1).astype(F32) * (2.0 / KX)
+        freq_y = ((col * K + (place & (K - 1)) + 1) >> 1).astype(F32) * (2.0 / KY)
+        wave = 4.0 * (freq_x * freq_x + freq_y * freq_y)
+        lapl = jnp.concatenate([wave] * (NZ // LANES), axis=1) + eig_val[...].reshape(1, NZ)
+        return 1.0 + diffuse_buoy * lapl, 1.0 + diffuse_vel * lapl
+
+    @pl.loop(0, PAIRS // 2)
+    def _(p):
+        rows = pl.ds(pl.multiple_of(p * TWO, TWO), TWO)
+        diag_buoy, diag_vel = diagonals(p)
+        inverses[rows, :] = 1.0 / (diag_buoy * diag_vel + couple_buoy * couple_vel)
+
+    def result(f, p):
+        rows = pl.ds(pl.multiple_of(p * TWO, TWO), TWO)
+        return pltpu.make_async_copy(done.at[f, rows, :], (out_buoy, out_vel)[f].at[rows, :], done_s.at[f, p])
+
+    pl.loop(3, 5)(relay_fwd)
     relay_turned()
     swap.wait()
     strata = jnp.where(high == 0, strat[...], strat_in[...]).reshape(1, ZPART)
@@ -448,18 +468,19 @@
             rhs = (field[rows, :].astype(F32) + explicit_step * tend).astype(BF)
             modal.append(mm(rhs, eig_left[...]))
         modal_buoy, modal_vel = modal
-        place = p * TWO + lax.broadcasted_iota(jnp.int32, (TWO, LANES), 0)
-        freq_x = ((row * A + (place >> 6) + 1) >> 1).astype(F32) * (2.0 / KX)
-        freq_y = ((col * K + (place & (K - 1)) + 1) >> 1).astype(F32) * (2.0 / KY)
-        wave = 4.0 * (freq_x * freq_x + freq_y * freq_y)
-        lapl = jnp.concatenate([wave] * (NZ // LANES), axis=1) + eig_val[...].reshape(1, NZ)
-        diag_buoy = 1.0 + diffuse_buoy * lapl
-        diag_vel = 1.0 + diffuse_vel * lapl
-        inverse = 1.0 / (diag_buoy * diag_vel + couple_buoy * couple_vel)
+        diag_buoy, diag_vel = diagonals(p)
+        inverse = inverses[rows, :]
         solved_buoy = ((diag_vel * modal_buoy - couple_buoy * modal_vel) * inverse).astype(BF)
         solved_vel = ((diag_buoy * modal_vel + couple_vel * modal_buoy) * inverse).astype(BF)
-        out_buoy[rows, :] = mm(solved_buoy, eig_right[...]).astype(BF)
-        out_vel[rows, :] = mm(solved_vel, eig_right[...]).astype(BF)
+        done[0, rows, :] = mm(solved_buoy, eig_right[...]).astype(BF)
+        done[1, rows, :] = mm(solved_vel, eig_right[...]).astype(BF)
+        result(0, p).start()
+        result(1, p).start()
+
+    @pl.loop(0, PAIRS // 2)
+    def _(p):
+        result(0, p).wait()
+        result(1, p).wait()
 
     def nothing():
         pass
@@ -501,7 +522,7 @@
         kernel,
         out_shape=(shape, shape),
         in_specs=[vmem] * 4 + [hbm] * 3 + [vmem] * 2 + [hbm] * 2,
-        out_specs=(vmem, vmem),
+        out_specs=(hbm, hbm),
         scratch_shapes=[
             pltpu.VMEM((G, COLS, ZC, 2, PAIRS, LANES), BF),
             pltpu.VMEM((G, ZC, COLS, 2, PAIRS, LANES), BF),
@@ -516,6 +537,9 @@
             pltpu.VMEM((KX, 2 * YG), BF),
             pltpu.VMEM((XG, 2 * YG), BF),
             pltpu.VMEM((2, modes, NZ), F32),
+            pltpu.VMEM((modes, NZ), F32),
+            pltpu.VMEM((2, modes, NZ), BF),
+            dma((2, PAIRS // 2)),
             pltpu.VMEM((ZPART,), F32),
             pltpu.VMEM((ZG, NZ), BF),
             pltpu.VMEM((KY, YG), BF),

time: 163 us -> 162 us (level)
  no operation moved by 1% of the time
where the time goes in v8:
time: 162 us; the launch traced here: 160 us
  Pallas kernels  155 us (96%)
  local copies, waits for them, and re-layouts  3.98 us (2%)
    pallas_call x1, Pallas kernels, per_device(): pl.pallas_call(kernel, out_shape=(shape, shape), in_specs=[vmem] * 4 + [h...  155 us
    unnamed x4, local copies, waits for them, and re-layouts  3.98 us

profile of v8, /device:TPU:5, one launch (start us, length us, event | category | flops | bytes accessed | tf_op | source)
XLA Modules:
  0.0 159.5 jit_solution(13956712431093254986)
XLA Ops:
  0.6 154.9 %section.1 = (bf16[2048,384]{1,0:T(8,128)(2,1)}, bf16[2048,384]{1,0:T(8,128)(2,1)}) custom-call(bf16[2048,384]{1,0:T(8,128)(2,1)} %bitcast.6, bf16[2048,384]{1,0:T(8,128)(2,1)} %bitcast.7, bf16[3,192,384]{2,1,0:T(8,128)(2,1)} %constant.10.clone.lift, bf16[3,192,384]{2,1,0:T(8,128)(2,1)} %constant.11.clone.slope, bf16[576,384]{1,0:T(8,128)(2,1)} %constant.12.clone.drop_in, ...), custom_call_target="tpu_custom_call" | custom-call | tf_op jit(solution)/shard_map/section/pallas_call | solution.py:521
  155.6 0.0 copy-start
  155.6 2.8 %copy.15 = bf16[32,64,384]{2,1,0:T(8,128)(2,1)} copy(bf16[32,64,384]{2,1,0:T(8,128)(2,1)} %bitcast.5) | data formatting | bytes 3145728
  158.4 0.0 copy-done
  158.4 1.1 copy.16
Async XLA Ops:
  155.6 2.8 %copy-start = (bf16[2048,384]{1,0:T(8,128)(2,1)S(1)}, bf16[2048,384]{1,0:T(8,128)(2,1)}, u32[]{:S(2)}) copy-start(bf16[2048,384]{1,0:T(8,128)(2,1)} %get-tuple-element.5) | copy-start | bytes 4718596

commit v9 on v8

--- a/solution.py
+++ b/solution.py
@@ -373,6 +373,7 @@
 
         @pl.when(m == TURN)
         def _():
+            pl.loop(0, 2)(relay_back)
             for h in range(2):
                 others(col, COLS, lambda s: hop_in(h, s).wait_recv())
                 hop_own(h).wait()
@@ -413,7 +414,7 @@
 
         @pl.when(m == last - 1)
         def _():
-            pl.loop(0, 2)(relay_back)
+            pl.loop(2, 4)(relay_back)
 
     def gather(first, last, f, start):
         @pl.loop(first, last)
@@ -434,7 +435,7 @@
             others(part, COLS, lambda q: col_back_in(g, q).wait_recv())
             col_back_own(g).wait()
 
-    pl.loop(2, ENDS[0] + 2)(relay_back)
+    pl.loop(4, ENDS[0] + 2)(relay_back)
     wait_modes(0, ENDS[0])
     for f in range(2):
         gather(0, ENDS[0], f, 0)

time: 162 us -> 160 us (0.988); the launches traced: 160 us -> 160 us
  no operation moved by 1% of the time
where the time goes in v9:
time: 160 us
  Pallas kernels  155 us (97%)
  local copies, waits for them, and re-layouts  3.98 us (2%)
    pallas_call x1, Pallas kernels, per_device(): pl.pallas_call(kernel, out_shape=(shape, shape), in_specs=[vmem] * 4 + [h...  155 us
    unnamed x4, local copies, waits for them, and re-layouts  3.98 us

profile of v9, /device:TPU:5, one launch (start us, length us, event | category | flops | bytes accessed | tf_op | source)
XLA Modules:
  0.0 160.1 jit_solution(580561735179985812)
XLA Ops:
  0.6 155.4 %section.1 = (bf16[2048,384]{1,0:T(8,128)(2,1)}, bf16[2048,384]{1,0:T(8,128)(2,1)}) custom-call(bf16[2048,384]{1,0:T(8,128)(2,1)} %bitcast.6, bf16[2048,384]{1,0:T(8,128)(2,1)} %bitcast.7, bf16[3,192,384]{2,1,0:T(8,128)(2,1)} %constant.10.clone.lift, bf16[3,192,384]{2,1,0:T(8,128)(2,1)} %constant.11.clone.slope, bf16[576,384]{1,0:T(8,128)(2,1)} %constant.12.clone.drop_in, ...), custom_call_target="tpu_custom_call" | custom-call | tf_op jit(solution)/shard_map/section/pallas_call | solution.py:522
  156.1 0.0 copy-start
  156.1 2.8 %copy.15 = bf16[32,64,384]{2,1,0:T(8,128)(2,1)} copy(bf16[32,64,384]{2,1,0:T(8,128)(2,1)} %bitcast.5) | data formatting | bytes 3145728
  158.9 0.0 copy-done
  158.9 1.1 copy.16
Async XLA Ops:
  156.1 2.8 %copy-start = (bf16[2048,384]{1,0:T(8,128)(2,1)S(1)}, bf16[2048,384]{1,0:T(8,128)(2,1)}, u32[]{:S(2)}) copy-start(bf16[2048,384]{1,0:T(8,128)(2,1)} %get-tuple-element.5) | copy-start | bytes 4718596

commit v10 on v9

--- a/solution.py
+++ b/solution.py
@@ -35,8 +35,7 @@
 SIZE = ZC * PAIRS
 TWO = 2 * LANES
 TALL = 4 * COLS * SIZE
-ORDER = (0, 6, 7, 1, 2, 3, 4, 5, 8)
-TURN = 3
+ORDER = (0, 4, 5, 1, 6, 7, 2, 3, 8)
 ENDS = (4, 8, 9)
 BF = jnp.bfloat16
 F32 = jnp.float32
@@ -198,34 +197,38 @@
         chips(1 - core, here, there)
 
     def turn_out(g, t):
+        m = g // 2
         return remote(
-            lifted.at[g, t // 2], arrived.at[2 * TURN + high, row % 8], turn_s.at[g % 2, t // 2], turn_r.at[row], row_of(t)
+            lifted.at[g, t // 2], arrived.at[2 * m + high, row % 8], turn_s.at[g - 4, t // 2], turn_r.at[m - 2, row], row_of(t)
         )
 
     def turn_own(g):
-        return pltpu.make_async_copy(lifted.at[g, chip], arrived.at[2 * TURN + high, row % 8], turn_r.at[row])
-
-    def turn_in(t):
-        block = arrived.at[2 * TURN + t // 8, t % 8]
-        return remote(block, block, turn_s.at[0, 0], turn_r.at[t], row_of(t))
-
-    def landing(h, s):
-        return planes.at[TURN, h * 8 : (h + 1) * 8, (s // 2) * 2 + (s % 2 + high + h) % 2]
-
-    def hop(h, q):
-        return remote(arrived.at[2 * TURN + h, :, q], landing(h, col), hop_s.at[h, q], hop_r.at[h, col], col_of(q))
-
-    def hop_in(h, s):
-        return remote(landing(h, s), landing(h, s), hop_s.at[h, s], hop_r.at[h, s], col_of(0))
-
-    def hop_own(h):
-        return pltpu.make_async_copy(arrived.at[2 * TURN + h, :, part], landing(h, col), hop_r.at[h, col])
-
-    def relay_turned():
-        members(lambda: turn_own(2 * TURN).wait(), lambda t: turn_in(t).wait_recv())
+        m = g // 2
+        return pltpu.make_async_copy(lifted.at[g, chip], arrived.at[2 * m + high, row % 8], turn_r.at[m - 2, row])
+
+    def turn_in(m, t):
+        block = arrived.at[2 * m + t // 8, t % 8]
+        return remote(block, block, turn_s.at[0, 0], turn_r.at[m - 2, t], row_of(t))
+
+    def landing(m, h, s):
+        return planes.at[m, h * 8 : (h + 1) * 8, (s // 2) * 2 + (s % 2 + high + h) % 2]
+
+    def hop(m, h, q):
+        return remote(
+            arrived.at[2 * m + h, :, q], landing(m, h, col), hop_s.at[m - 2, h, q], hop_r.at[m - 2, h, col], col_of(q)
+        )
+
+    def hop_in(m, h, s):
+        return remote(landing(m, h, s), landing(m, h, s), hop_s.at[m - 2, h, s], hop_r.at[m - 2, h, s], col_of(0))
+
+    def hop_own(m, h):
+        return pltpu.make_async_copy(arrived.at[2 * m + h, :, part], landing(m, h, col), hop_r.at[m - 2, h, col])
+
+    def relay_turned(m):
+        members(lambda: turn_own(2 * m).wait(), lambda t: turn_in(m, t).wait_recv())
         for h in range(2):
-            others(part, COLS, lambda q: hop(h, q).start())
-            hop_own(h).start()
+            others(part, COLS, lambda q: hop(m, h, q).start())
+            hop_own(m, h).start()
 
     def relay_fwd(g):
         others(col, COLS, lambda s: col_fwd_in(g, s).wait_recv())
@@ -242,7 +245,8 @@
     chunks = G // PASSES
 
     def chunk_at(i):
-        return jnp.where(i == 0, 0, jnp.where(i < 3, i + 5, jnp.where(i < 8, i - 2, 8)))
+        late = jnp.where(i < 6, i + 2, jnp.where(i < 8, i - 4, 8))
+        return jnp.where(i == 0, 0, jnp.where(i < 3, i + 3, jnp.where(i == 3, 1, late)))
 
     def to_points(u):
         for f, (table, field) in enumerate(((lift, vel), (slope, buoy))):
@@ -260,11 +264,11 @@
                 block = tall[rows, :].astype(BF).reshape(ZC, PAIRS, LANES)
                 g, q = chunk_at(u * chunks + i // COLS), i % COLS
 
-                @pl.when(g // 2 != TURN)
+                @pl.when(g // 4 != 1)
                 def _():
                     lifted[g, q, :, f] = block
 
-                @pl.when(g // 2 == TURN)
+                @pl.when(g // 4 == 1)
                 def _():
                     lifted[g, :, q, f] = block
 
@@ -273,12 +277,12 @@
         def _(i):
             g = chunk_at(i)
 
-            @pl.when(g // 2 != TURN)
+            @pl.when(g // 4 != 1)
             def _():
                 others(part, COLS, lambda q: col_fwd(g, q).start())
                 col_fwd_own(g).start()
 
-            @pl.when(g // 2 == TURN)
+            @pl.when(g // 4 == 1)
             def _():
                 chips(g % 2, lambda: turn_own(g).start(), lambda t: turn_out(g, t).start())
 
@@ -354,8 +358,11 @@
         rows = pl.ds(pl.multiple_of(p * TWO, TWO), TWO)
         return pltpu.make_async_copy(done.at[f, rows, :], (out_buoy, out_vel)[f].at[rows, :], done_s.at[f, p])
 
-    pl.loop(3, 5)(relay_fwd)
-    relay_turned()
+    @pl.loop(2, 4)
+    def _(m):
+        relay_turned(m)
+        pl.when(m == 2)(lambda: relay_fwd(3))
+
     swap.wait()
     strata = jnp.where(high == 0, strat[...], strat_in[...]).reshape(1, ZPART)
     level_of = lax.broadcasted_iota(jnp.int32, (1, ZPART), 1)
@@ -367,23 +374,24 @@
     def _(m):
         chunk = 2 * m + core
 
-        @pl.when(m != TURN)
+        pl.when(m == last - 1)(lambda: pl.loop(0, 2)(relay_back))
+
+        @pl.when(m // 2 != 1)
         def _():
             members(lambda: row_fwd_own(2 * m).wait(), lambda t: row_fwd_in(m, t).wait_recv())
 
-        @pl.when(m == TURN)
+        @pl.when(m // 2 == 1)
         def _():
-            pl.loop(0, 2)(relay_back)
             for h in range(2):
-                others(col, COLS, lambda s: hop_in(h, s).wait_recv())
-                hop_own(h).wait()
+                others(col, COLS, lambda s: hop_in(m, h, s).wait_recv())
+                hop_own(m, h).wait()
 
         for f in range(2):
             left = jnp.concatenate([planes[m, :, s, f].reshape(half, LANES) for s in range(COLS)], axis=1)
             for a in range(2):
                 middle[a * half : (a + 1) * half, f * YG : (f + 1) * YG] = mm(left, wide_eval[a]).astype(BF)
 
-        pl.when(m < 2)(lambda: relay_fwd(5 + 3 * m))
+        pl.when(m == 0)(lambda: relay_fwd(G - 1))
 
         level = jnp.sum(jnp.where(level_of == chip * G + chunk, strata, 0.0), axis=1, keepdims=True)
         tile = XG // 3
@@ -486,16 +494,18 @@
     def nothing():
         pass
 
-    for h in range(2):
-        others(part, COLS, lambda q: hop(h, q).wait_send())
+    @pl.loop(2, 4)
+    def _(m):
+        for h in range(2):
+            others(part, COLS, lambda q: hop(m, h, q).wait_send())
 
     @pl.loop(0, G)
     def _(g):
-        @pl.when(g // 2 != TURN)
+        @pl.when(g // 4 != 1)
         def _():
             others(part, COLS, lambda q: col_fwd(g, q).wait_send())
 
-        @pl.when(g // 2 == TURN)
+        @pl.when(g // 4 == 1)
         def _():
             chips(g % 2, nothing, lambda t: turn_out(g, t).wait_send())
 
@@ -503,7 +513,7 @@
 
     @pl.loop(0, last)
     def _(m):
-        pl.when(m != TURN)(lambda: members(nothing, lambda t: row_fwd(2 * m, t).wait_send()))
+        pl.when(m // 2 != 1)(lambda: members(nothing, lambda t: row_fwd(2 * m, t).wait_send()))
 
     @pl.loop(0, last + 1 - core)
     def _(m):
@@ -547,7 +557,7 @@
             pltpu.VMEM((YG, KY), BF),
             pltpu.VMEM((NZ, NZ), BF),
             pltpu.VMEM((NZ, NZ), BF),
-            dma((5,)), dma((2, ZC)), dma((ROWS,)), dma((2, COLS)), dma((2, COLS)),
+            dma((5,)), dma((4, ZC)), dma((2, ROWS)), dma((2, 2, COLS)), dma((2, 2, COLS)),
             dma((G, COLS)), dma((G, COLS)), dma((G // 2 + 1, ROWS)), dma((G // 2 + 1, ROWS)),
             dma((G // 2 + 1, ROWS)), dma((G, ZC)), dma((G, COLS)), dma((G, COLS)),
             dma, dma,

time: 160 us -> 159 us (level)
    pallas_call x1, Pallas kernels: 155 us -> 154 us  [per_device(): pl.pallas_call(kernel, out_shape=(shape, shape), in_specs=[vmem] * 4 + [h...]
where the time goes in v10:
time: 159 us; the launch traced here: 158 us
  Pallas kernels  154 us (97%)
  local copies, waits for them, and re-layouts  3.98 us (3%)
    pallas_call x1, Pallas kernels, per_device(): pl.pallas_call(kernel, out_shape=(shape, shape), in_specs=[vmem] * 4 + [h...  154 us
    unnamed x4, local copies, waits for them, and re-layouts  3.98 us

profile of v10, /device:TPU:5, one launch (start us, length us, event | category | flops | bytes accessed | tf_op | source)
XLA Modules:
  0.0 158.4 jit_solution(6379470321723638104)
XLA Ops:
  0.6 153.8 %section.1 = (bf16[2048,384]{1,0:T(8,128)(2,1)}, bf16[2048,384]{1,0:T(8,128)(2,1)}) custom-call(bf16[2048,384]{1,0:T(8,128)(2,1)} %bitcast.6, bf16[2048,384]{1,0:T(8,128)(2,1)} %bitcast.7, bf16[3,192,384]{2,1,0:T(8,128)(2,1)} %constant.10.clone.lift, bf16[3,192,384]{2,1,0:T(8,128)(2,1)} %constant.11.clone.slope, bf16[576,384]{1,0:T(8,128)(2,1)} %constant.12.clone.drop_in, ...), custom_call_target="tpu_custom_call" | custom-call | tf_op jit(solution)/shard_map/section/pallas_call | solution.py:532
  154.4 0.0 copy-start
  154.4 2.8 %copy.15 = bf16[32,64,384]{2,1,0:T(8,128)(2,1)} copy(bf16[32,64,384]{2,1,0:T(8,128)(2,1)} %bitcast.5) | data formatting | bytes 3145728
  157.2 0.0 copy-done
  157.2 1.1 copy.16
Async XLA Ops:
  154.4 2.8 %copy-start = (bf16[2048,384]{1,0:T(8,128)(2,1)S(1)}, bf16[2048,384]{1,0:T(8,128)(2,1)}, u32[]{:S(2)}) copy-start(bf16[2048,384]{1,0:T(8,128)(2,1)} %get-tuple-element.5) | copy-start | bytes 4718596

commit v11 on v10

--- a/solution.py
+++ b/solution.py
@@ -443,7 +443,7 @@
             others(part, COLS, lambda q: col_back_in(g, q).wait_recv())
             col_back_own(g).wait()
 
-    pl.loop(4, ENDS[0] + 2)(relay_back)
+    pl.loop(4, G - 1)(relay_back)
     wait_modes(0, ENDS[0])
     for f in range(2):
         gather(0, ENDS[0], f, 0)
@@ -453,7 +453,7 @@
             rows = pl.ds(pl.multiple_of(p * TWO, TWO), TWO)
             partial[f, rows, :] = tendency(0, ENDS[0], p, 0)
 
-    pl.loop(ENDS[0] + 2, G)(relay_back)
+    relay_back(G - 1)
     wait_modes(ENDS[0], ENDS[1])
     for f in range(2):
         gather(ENDS[0], ENDS[1], f, 0)

time: 159 us -> 159 us (level)
  no operation moved by 1% of the time
where the time goes in v11:
time: 159 us
  Pallas kernels  154 us (97%)
  local copies, waits for them, and re-layouts  3.98 us (3%)
    pallas_call x1, Pallas kernels, per_device(): pl.pallas_call(kernel, out_shape=(shape, shape), in_specs=[vmem] * 4 + [h...  154 us
    unnamed x4, local copies, waits for them, and re-layouts  3.98 us

profile of v11, /device:TPU:5, one launch (start us, length us, event | category | flops | bytes accessed | tf_op | source)
XLA Modules:
  0.0 158.6 jit_solution(12219779420560961885)
XLA Ops:
  0.6 153.9 %section.1 = (bf16[2048,384]{1,0:T(8,128)(2,1)}, bf16[2048,384]{1,0:T(8,128)(2,1)}) custom-call(bf16[2048,384]{1,0:T(8,128)(2,1)} %bitcast.6, bf16[2048,384]{1,0:T(8,128)(2,1)} %bitcast.7, bf16[3,192,384]{2,1,0:T(8,128)(2,1)} %constant.10.clone.lift, bf16[3,192,384]{2,1,0:T(8,128)(2,1)} %constant.11.clone.slope, bf16[576,384]{1,0:T(8,128)(2,1)} %constant.12.clone.drop_in, ...), custom_call_target="tpu_custom_call" | custom-call | tf_op jit(solution)/shard_map/section/pallas_call | solution.py:532
  154.6 0.0 copy-start
  154.6 2.8 %copy.15 = bf16[32,64,384]{2,1,0:T(8,128)(2,1)} copy(bf16[32,64,384]{2,1,0:T(8,128)(2,1)} %bitcast.5) | data formatting | bytes 3145728
  157.4 0.0 copy-done
  157.4 1.1 copy.16
Async XLA Ops:
  154.6 2.8 %copy-start = (bf16[2048,384]{1,0:T(8,128)(2,1)S(1)}, bf16[2048,384]{1,0:T(8,128)(2,1)}, u32[]{:S(2)}) copy-start(bf16[2048,384]{1,0:T(8,128)(2,1)} %get-tuple-element.5) | copy-start | bytes 4718596
